TPU v7x, 256 devices: a whole 4x4x8 slice. The times are simulated.
256 devices in a mesh: dp: 16 (over x, y_hi, core), space: 16 (over y_lo, z).
Axes of the slice: x: 4, y: 4 (y_hi: 2, y_lo: 2; y = y_hi * 2 + y_lo), z: 8, core: 2. Of those that a mesh axis runs over, the one named last changes fastest.
Arguments:
- state_field: bfloat16 [16, 160, 320, 128], P('dp', 'space'), may hold values from -6 to 6
- cotangent: bfloat16 [16, 160, 320, 128], P('dp', 'space'), may hold values from -6 to 6
- fire_cells: int32 [16, 256], P('dp'), may hold values from 0 to 51199
- fire_kinds: int32 [16, 256], P('dp'), may hold values from 0 to 7
- fire_heat: float32 [16, 256], P('dp'), may hold values from 0.1 to 2
- forcing_table: bfloat16 [8, 128], replicated, may hold values from -6 to 6
- spectral_weight: bfloat16 [2, 80, 2, 128, 128], P(None, 'space'), may hold values from -0.375 to 0.375
- skip_weight: bfloat16 [128, 128], replicated, may hold values from -0.5 to 0.5
- up_weight: bfloat16 [128, 256], replicated, may hold values from -0.5 to 0.5
- down_weight: bfloat16 [256, 128], replicated, may hold values from -0.375 to 0.375
Outputs:
- grad_field: bfloat16 [16, 160, 320, 128], P('dp', 'space')
- grad_spectral: float32 [2, 80, 2, 128, 128], P(None, 'space')
- grad_skip: float32 [128, 128], replicated
- grad_up: float32 [128, 256], replicated
- grad_down: float32 [256, 128], replicated
- grad_table: float32 [8, 128], replicated
All inputs are finite; a program needn't handle non-finite values.
Results may differ from a plain program's by a relative error of at most 0.03.
Values may be sent and summed in bfloat16 or wider, within the bound.
A program may use at most 128 MiB of HBM per device.

v0:
```python
import jax
import jax.numpy as jnp
import numpy as np
from jax import lax
from jax.sharding import PartitionSpec as P

LATITUDE_ROWS = 160
NLON = 320
LMAX = 160
ZONAL_MODES_KEPT = 160
CHAN = 128
HIDDEN_SIZE = 256
FORCE = 8


EPSILON = 1e-06


def normalize(values):
    centre = values - jnp.mean(values, axis=-1, keepdims=True)
    variance = jnp.mean(centre * centre, axis=-1, keepdims=True)
    return centre * lax.rsqrt(variance + EPSILON)


def smooth(values):
    return jax.nn.gelu(values, approximate=True)


def fourier_tables(mode_ids, point_total):
    wavenumber = mode_ids[:, None]
    position = jnp.arange(point_total, dtype=jnp.int32)[None, :]
    angles = 2.0 * jnp.pi / point_total * (wavenumber * position % point_total).astype(jnp.float32)
    cosine = jnp.cos(angles)
    sine_wave = jnp.sin(angles)
    factor = jnp.where(wavenumber == 0, 1.0, 2.0).astype(jnp.float32)
    analysis = jnp.stack([cosine / point_total, -sine_wave / point_total], axis=1).astype(
        jnp.bfloat16
    )
    synthesis = jnp.stack([factor * cosine, -factor * sine_wave], axis=1).astype(jnp.bfloat16)
    return (analysis, synthesis)


def legendre_tables(order_ids):
    mode_total = order_ids.shape[0]
    orders = order_ids.astype(jnp.float32)[:, None]
    colatitude = (
        jnp.pi
        * (jnp.arange(LATITUDE_ROWS, dtype=jnp.int32).astype(jnp.float32) + 0.5)
        / LATITUDE_ROWS
    )
    cos_lat = jnp.cos(colatitude)[None, :]
    sin_lat = jnp.sin(colatitude)[None, :]
    quadrature = 2.0 * jnp.pi * jnp.pi / LATITUDE_ROWS * sin_lat
    log_start = (
        0.5 * jnp.log((2.0 * orders + 1.0) / (4.0 * jnp.pi))
        + 0.5 * (lax.lgamma(orders + 0.5) - lax.lgamma(orders + 1.0))
        - 0.25 * jnp.log(jnp.pi)
    )
    diagonal = jnp.exp(log_start + orders * jnp.log(sin_lat))

    def advance(state_pair, degree):
        previous, before = state_pair
        as_float = degree.astype(jnp.float32)
        upward = jnp.sqrt(
            jnp.maximum(4.0 * as_float * as_float - 1.0, 1.0)
            / jnp.maximum(as_float * as_float - orders * orders, 1.0)
        )
        lower = as_float - 1.0
        downward = jnp.sqrt(
            jnp.maximum(lower * lower - orders * orders, 0.0)
            / jnp.maximum(4.0 * lower * lower - 1.0, 1.0)
        )
        recurred = upward * (cos_lat * previous - downward * before)
        current = jnp.where(
            as_float == orders, diagonal, jnp.where(as_float > orders, recurred, 0.0)
        )
        return (
            (current, previous),
            (current.astype(jnp.bfloat16), (current * quadrature).astype(jnp.bfloat16)),
        )

    zeros_start = jnp.zeros((mode_total, LATITUDE_ROWS), jnp.float32)
    final_pair, tables = lax.scan(
        advance, (zeros_start, zeros_start), jnp.arange(LMAX, dtype=jnp.int32), unroll=16
    )
    return tables


def mix_matrix(weights):
    real_part = weights[:, 0]
    imag_part = weights[:, 1]
    top_rows = jnp.concatenate([real_part, imag_part], axis=-1)
    bottom = jnp.concatenate([-imag_part, real_part], axis=-1)
    return jnp.concatenate([top_rows, bottom], axis=1)


def mix_gradient(harmonic_coefficients, mixed_gradient):
    degree_count, mode_count, part_count, chan_count = harmonic_coefficients.shape
    flattened = harmonic_coefficients.reshape(degree_count, mode_count * part_count, chan_count)
    turned = jnp.stack([mixed_gradient[:, :, 1], -mixed_gradient[:, :, 0]], axis=2)
    paired = jnp.concatenate(
        [mixed_gradient.reshape(flattened.shape), turned.reshape(flattened.shape)], axis=-1
    )
    outer_prod = jnp.einsum("lpr,lps->lrs", flattened, paired, preferred_element_type=jnp.float32)
    return jnp.transpose(outer_prod.reshape(degree_count, chan_count, 2, chan_count), (0, 2, 1, 3))


def fold_orders(group_count, half_block, total_count):
    starts = np.arange(group_count)[:, None] * half_block
    offsets = np.arange(half_block)[None, :]
    return np.concatenate([starts + offsets, total_count - 1 - starts - offsets], axis=1)


def triangle_tables(group_count, half_block, total_count):
    block_width = 2 * half_block
    block_area = block_width * block_width
    orders = fold_orders(group_count, half_block, total_count)
    kept_mask = orders[None, :, :, None] >= orders[:, None, None, :]
    flat_keep = kept_mask.reshape(group_count, group_count, block_area)
    rank_table = np.cumsum(flat_keep, axis=2) - 1
    slot_count = int(flat_keep.sum(axis=2).max())
    zero_grid = np.zeros(flat_keep.shape, np.int64)
    sender = (np.arange(group_count)[:, None, None] + zero_grid)[flat_keep]
    target = (np.arange(group_count)[None, :, None] + zero_grid)[flat_keep]
    pairs = (np.arange(block_area)[None, None, :] + zero_grid)[flat_keep]
    places = rank_table[sender, target, pairs]
    row_index = pairs // block_width
    col_index = pairs % block_width
    send_forward = np.full(
        (group_count, group_count * slot_count), total_count * block_width, np.int32
    )
    send_forward[sender, target * slot_count + places] = target * block_area + pairs
    recv_forward = np.full(
        (group_count, block_width * total_count), group_count * slot_count, np.int32
    )
    recv_forward[target, row_index * total_count + sender * block_width + col_index] = (
        sender * slot_count + places
    )
    send_backward = np.full(
        (group_count, group_count * slot_count), block_width * total_count, np.int32
    )
    send_backward[target, sender * slot_count + places] = (
        row_index * total_count + sender * block_width + col_index
    )
    recv_backward = np.full(
        (group_count, total_count * block_width), group_count * slot_count, np.int32
    )
    recv_backward[sender, target * block_area + pairs] = target * slot_count + places
    return (orders, send_forward, recv_forward, send_backward, recv_backward)


def to_modes(field_grid, weights_table):
    return jnp.einsum(
        "mpk,jkc->mjpc", weights_table, field_grid, preferred_element_type=jnp.float32
    ).astype(jnp.bfloat16)


def to_field(spectrum_values, weights_table):
    return jnp.einsum(
        "mpk,mjpc->jkc", weights_table, spectrum_values, preferred_element_type=jnp.float32
    )


def analyse_degrees(spectrum_values, legendre):
    mode_count, row_count, part_count, chan_count = spectrum_values.shape
    result = jnp.einsum(
        "vbz,bzq->vbq",
        legendre,
        spectrum_values.reshape(mode_count, row_count, part_count * chan_count),
        preferred_element_type=jnp.float32,
    )
    return result.astype(jnp.bfloat16).reshape(
        legendre.shape[0], mode_count, part_count, chan_count
    )


def synthesise_rows(harmonic_coefficients, legendre):
    degree_count, mode_count, part_count, chan_count = harmonic_coefficients.shape
    result = jnp.einsum(
        "cfg,cft->fgt",
        legendre,
        harmonic_coefficients.reshape(degree_count, mode_count, part_count * chan_count),
        preferred_element_type=jnp.float32,
    )
    return result.astype(jnp.bfloat16).reshape(
        mode_count, legendre.shape[2], part_count, chan_count
    )


def to_degrees(values):
    result = lax.all_to_all(values, "space", split_axis=0, concat_axis=1, tiled=True)
    return result


def from_degrees(values):
    result = lax.all_to_all(values, "space", split_axis=1, concat_axis=0, tiled=True)
    return result


def to_spectral(values):
    return lax.all_to_all(values, "space", split_axis=0, concat_axis=1, tiled=True)


def to_rows(values):
    return lax.all_to_all(values, "space", split_axis=1, concat_axis=0, tiled=True)


def shards(
    state_field,
    cotangent,
    fire_cells,
    fire_kinds,
    fire_heat,
    forcing_table,
    spectral_weight,
    skip_weight,
    up_weight,
    down_weight,
):
    group_size = lax.axis_size("space")
    device_index = lax.axis_index("space")
    lat_local = state_field.shape[1]
    cell_count = lat_local * NLON
    half_block = spectral_weight.shape[1]
    degree_local = 2 * half_block
    doubled_channels = 2 * CHAN
    fold_table, send_forward, recv_forward, send_backward, recv_backward = triangle_tables(
        group_size, half_block, ZONAL_MODES_KEPT
    )
    mode_order = jnp.asarray(fold_table.reshape(-1), jnp.int32)
    analysis, synthesis = fourier_tables(mode_order, NLON)
    local_orders = jnp.asarray(fold_table, jnp.int32)[device_index]
    plain_full, weighted_full = legendre_tables(local_orders)
    plain_table = jnp.take(plain_full, mode_order, axis=0)
    weighted = jnp.take(weighted_full, mode_order, axis=0)
    mixing = mix_matrix(spectral_weight.reshape(degree_local, 2, CHAN, CHAN))
    table_wide = forcing_table.astype(jnp.float32)
    kind_range = jnp.arange(FORCE, dtype=jnp.int32)
    totals = (
        jnp.zeros((degree_local, 2, CHAN, CHAN), jnp.float32),
        jnp.zeros((CHAN, CHAN), jnp.float32),
        jnp.zeros((CHAN, HIDDEN_SIZE), jnp.float32),
        jnp.zeros((HIDDEN_SIZE, CHAN), jnp.float32),
        jnp.zeros((FORCE, CHAN), jnp.float32),
    )
    flat_in = state_field[0].astype(jnp.float32).reshape(cell_count, CHAN)
    selector = (fire_kinds[0][:, None] == kind_range[None, :]).astype(jnp.float32)
    heat_values = fire_heat[0]
    rows_added = heat_values[:, None] * jnp.dot(
        selector, table_wide, precision=lax.Precision.HIGHEST
    )
    offset = fire_cells[0] - device_index * cell_count
    inside = (offset >= 0) & (offset < cell_count)
    local_slot = jnp.clip(offset, 0, cell_count - 1)
    forced = flat_in.at[local_slot].add(jnp.where(inside[:, None], rows_added, 0.0))
    normed = normalize(forced).astype(jnp.bfloat16)
    spectrum_values = to_spectral(to_modes(normed.reshape(lat_local, NLON, CHAN), analysis))
    harmonic_coefficients = to_degrees(analyse_degrees(spectrum_values, weighted))
    mixed_coefficients = (
        jnp.einsum(
            "acw,awf->acf",
            harmonic_coefficients.reshape(degree_local, ZONAL_MODES_KEPT, doubled_channels),
            mixing,
            preferred_element_type=jnp.float32,
        )
        .astype(jnp.bfloat16)
        .reshape(harmonic_coefficients.shape)
    )
    returned_rows = synthesise_rows(from_degrees(mixed_coefficients), plain_table)
    filtered = to_field(to_rows(returned_rows), synthesis).reshape(cell_count, CHAN)
    inner_sum = filtered + jnp.dot(normed, skip_weight, preferred_element_type=jnp.float32)
    activated = smooth(inner_sum)
    second = normalize(activated).astype(jnp.bfloat16)
    upper = jnp.dot(second, up_weight, preferred_element_type=jnp.float32)
    hidden = smooth(upper).astype(jnp.bfloat16)
    incoming = cotangent[0].reshape(cell_count, CHAN)
    grad_hidden = jnp.dot(incoming, down_weight.T, preferred_element_type=jnp.float32)
    grad_down = jnp.dot(hidden.T, incoming, preferred_element_type=jnp.float32)
    grad_upper = jax.vjp(smooth, upper)[1](grad_hidden)[0].astype(jnp.bfloat16)
    grad_second = jnp.dot(grad_upper, up_weight.T, preferred_element_type=jnp.float32)
    grad_up = jnp.dot(second.T, grad_upper, preferred_element_type=jnp.float32)
    grad_activated = jax.vjp(normalize, activated)[1](grad_second)[0]
    grad_inner = jax.vjp(smooth, inner_sum)[1](grad_activated)[0].astype(jnp.bfloat16)
    grad_skip = jnp.dot(normed.T, grad_inner, preferred_element_type=jnp.float32)
    grad_normed = jnp.dot(grad_inner, skip_weight.T, preferred_element_type=jnp.float32)
    spectrum_gradient = to_spectral(to_modes(grad_inner.reshape(lat_local, NLON, CHAN), synthesis))
    mixed_gradient = to_degrees(analyse_degrees(spectrum_gradient, plain_table))
    coefficient_gradient = (
        jnp.einsum(
            "dfb,dub->dfu",
            mixed_gradient.reshape(degree_local, ZONAL_MODES_KEPT, doubled_channels),
            mixing,
            preferred_element_type=jnp.float32,
        )
        .astype(jnp.bfloat16)
        .reshape(mixed_gradient.shape)
    )
    grad_degree = mix_gradient(harmonic_coefficients, mixed_gradient)
    gradient_returned = synthesise_rows(from_degrees(coefficient_gradient), weighted)
    grad_normed = grad_normed + to_field(to_rows(gradient_returned), analysis).reshape(
        cell_count, CHAN
    )
    grad_forced = incoming.astype(jnp.float32) + jax.vjp(normalize, forced)[1](grad_normed)[0]
    picked = jnp.take(grad_forced, local_slot, axis=0) * inside[:, None].astype(jnp.float32)
    grad_table = jnp.dot(selector.T, heat_values[:, None] * picked, precision=lax.Precision.HIGHEST)
    grads = (grad_degree, grad_skip, grad_up, grad_down, grad_table)
    totals = jax.tree.map(jnp.add, totals, grads)
    outputs = [grad_forced.astype(jnp.bfloat16).reshape(lat_local, NLON, CHAN)]
    grad_field = jnp.stack(outputs)
    spectral_local = totals[0].reshape(spectral_weight.shape)
    spectral_total = lax.psum(spectral_local.astype(jnp.bfloat16), "dp").astype(jnp.float32)
    skip_total, up_total, down_total, table_total = lax.psum(
        (totals[1], totals[2], totals[3], totals[4]), ("dp", "space")
    )
    return (grad_field, spectral_total, skip_total, up_total, down_total, table_total)


def solution(mesh):
    return jax.shard_map(
        shards,
        mesh=mesh,
        in_specs=(
            P("dp", "space", None, None),
            P("dp", "space", None, None),
            P("dp", None),
            P("dp", None),
            P("dp", None),
            P(),
            P(None, "space", None, None, None),
            P(),
            P(),
            P(),
        ),
        out_specs=(
            P("dp", "space", None, None),
            P(None, "space", None, None, None),
            P(),
            P(),
            P(),
            P(),
        ),
        check_vma=False,
    )
```

profile of v0, /device:TPU:1, one launch (start us, length us, event | category | flops | bytes accessed | tf_op | source)
XLA Modules:
  0.0 849.6 jit_solution(4225850891564338054)
XLA Ops:
  21.1 10.5 %all-to-all-start = ((bf16[160,10,2,128]{3,2,1,0:T(2,128)(2,1)}), bf16[160,10,2,128]{3,2,1,0:T(2,128)(2,1)S(1)}, u32[]{:S(2)}, u32[]{:S(2)}) async-start(bf16[160,10,2,128]{3,2,1,0:T(2,128)(2,1)} %copy.64), calls=%async_computation | async-start | bytes 1638400 | tf_op jit(solution)/shard_map/all_to_all | solution.py:201
  33.8 135.3 %while.21 = (s32[]{:T(128)}, f32[10,160]{1,0:T(8,128)S(1)}, f32[10,160]{1,0:T(8,128)S(1)}, bf16[10,16,10,160]{3,2,1,0:T(8,128)(2,1)}, bf16[10,16,10,160]{3,2,1,0...) while((s32[]{:T(128)}, f32[10,160]{1,0:T(8,128)S(1)}, ...), condition=%wide.region_1.2_spmd.clone.clone, body=%wide.region_0.1_spmd.clone.clone.sunk | while | flops 288993 | bytes 1509868 | solution.py:83
  169.1 3.3 gather_fusion.2
  184.0 7.8 all-to-all-start.1
  193.6 17.8 %all-to-all-done.1 = bf16[160,10,2,128]{3,2,1,0:T(2,128)(2,1)S(1)} async-done(((bf16[160,10,2,128]{3,2,1,0:T(2,128)(2,1)}), bf16[160,10,2,128]{3,2,1,0:T(2,128)(2,1)S(1)}, u32[]{:S(2)}, u32[]{:S(2)}) %all-to-all-start.1) | async-done | bytes 819232 | tf_op jit(solution)/shard_map/all_to_all | solution.py:191
  218.8 6.7 all-to-all-start.2
  227.6 17.3 %all-to-all-done.2 = bf16[10,160,2,128]{3,2,0,1:T(2,128)(2,1)} async-done(((bf16[10,160,2,128]{3,2,0,1:T(2,128)(2,1)}), bf16[10,160,2,128]{3,2,0,1:T(2,128)(2,1)}, u32[]{:S(2)}, u32[]{:S(2)}) %all-to-all-start.2) | async-done | bytes 819232 | tf_op jit(solution)/shard_map/all_to_all | solution.py:196
  247.7 3.2 reshape.1631
  256.1 26.6 %all_to_all.129 = bf16[10,160,2,128]{3,2,0,1:T(2,128)(2,1)S(1)} all-to-all(bf16[10,160,2,128]{3,2,0,1:T(2,128)(2,1)S(1)} %copy.73), channel_id=1, replica_groups=mesh['dp'=16,'space'=16] {'space'}, dimensions={1} | all-to-all | bytes 1638400 | tf_op jit(solution)/shard_map/all_to_all | solution.py:205
  299.2 25.7 %all_to_all.130 = bf16[160,10,2,128]{3,2,1,0:T(2,128)(2,1)S(1)} all-to-all(bf16[160,10,2,128]{3,2,1,0:T(2,128)(2,1)S(1)} %copy.77), channel_id=1, replica_groups=mesh['dp'=16,'space'=16] {'space'}, dimensions={0} | all-to-all | bytes 1638400 | tf_op jit(solution)/shard_map/all_to_all | solution.py:201
  326.5 3.2 reshape.1635
  329.7 2.9 fusion.67
  337.1 25.6 %all_to_all.131 = bf16[160,10,2,128]{3,2,1,0:T(2,128)(2,1)S(1)} all-to-all(bf16[160,10,2,128]{3,2,1,0:T(2,128)(2,1)S(1)} %copy.80), channel_id=1, replica_groups=mesh['dp'=16,'space'=16] {'space'}, dimensions={0} | all-to-all | bytes 1638400 | tf_op jit(solution)/shard_map/all_to_all | solution.py:191
  364.2 3.2 reshape.1637
  367.4 3.1 convolution_convert_fusion
  375.8 6.0 all-to-all-start.6
  382.5 18.2 %all-to-all-done.6 = bf16[10,160,2,128]{3,2,0,1:T(2,128)(2,1)} async-done(((bf16[10,160,2,128]{3,2,0,1:T(2,128)(2,1)}), bf16[10,160,2,128]{3,2,0,1:T(2,128)(2,1)}, u32[]{:S(2)}, u32[]{:S(2)}) %all-to-all-start.6) | async-done | bytes 819232 | tf_op jit(solution)/shard_map/all_to_all | solution.py:196
  403.4 3.2 reshape.1639
  414.7 6.5 all-to-all-start.7
  421.3 4.5 fusion.114
  436.8 3.9 fusion.60
  440.7 141.4 %all-reduce.4.cloned.1.call-done = bf16[2,5,2,128,128]{4,3,2,1,0:T(8,128)(2,1)} async-done(((bf16[2,5,2,128,128]{4,3,2,1,0:T(8,128)(2,1)}), bf16[2,5,2,128,128]{4,3,2,1,0:T(8,128)(2,1)}) %all-reduce.4.cloned.1.call-update) | async-done | bytes 655376 | tf_op jit(solution)/shard_map/psum | solution.py:311
  592.3 78.9 %psum.39 = f32[8,128]{1,0:T(8,128)} all-reduce(f32[8,128]{1,0:T(8,128)S(1)} %fusion.82), channel_id=1, replica_groups=mesh['dp'=16,'space'=16] {'dp','space'}, use_global_device_ids=true, to_apply=%region_15.17 | all-reduce | flops 1024 | bytes 8192 | tf_op jit(solution)/shard_map/psum | solution.py:312
  671.2 166.7 %all-reduce.6.cloned.1.call-done = (f32[128,128]{1,0:T(8,128)}, f32[128,256]{1,0:T(8,128)}, f32[256,128]{1,0:T(8,128)}) async-done(((f32[128,128]{1,0:T(8,128)}, f32[128,256]{1,0:T(8,128)}, f32[256,128]{1,0:T(8,128)}), (f32[128,128]{1,0:T(8,128)}, f32[128,256]{1,0:T(8,128)}, f32[256,128]{1,0:T(8,128)})) %all-reduce.6.cloned.1.call-update) | async-done | bytes 327696 | tf_op jit(solution)/shard_map/psum | solution.py:312
  (437 shorter events, 144.2 us)
Async XLA Ops:
  7.2 279.2 %copy-start = (bf16[128,256]{1,0:T(8,128)(2,1)S(1)}, bf16[128,256]{1,0:T(8,128)(2,1)}, u32[]{:S(2)}) copy-start(bf16[128,256]{1,0:T(8,128)(2,1)} %param.24) | copy-start | bytes 196612
  7.2 2.7 copy-start.28
  7.2 2.7 copy-start.31
  7.2 2.7 copy-start.29
  21.1 153.9 %all-to-all-start = ((bf16[160,10,2,128]{3,2,1,0:T(2,128)(2,1)}), bf16[160,10,2,128]{3,2,1,0:T(2,128)(2,1)S(1)}, u32[]{:S(2)}, u32[]{:S(2)}) async-start(bf16[160,10,2,128]{3,2,1,0:T(2,128)(2,1)} %copy.64), calls=%async_computation | async-start | bytes 1638400 | tf_op jit(solution)/shard_map/all_to_all | solution.py:201
  175.0 4.1 copy-start.3
  184.0 7.8 copy-start.15
  184.0 27.4 %all-to-all-start.1 = ((bf16[160,10,2,128]{3,2,1,0:T(2,128)(2,1)}), bf16[160,10,2,128]{3,2,1,0:T(2,128)(2,1)S(1)}, u32[]{:S(2)}, u32[]{:S(2)}) async-start(bf16[160,10,2,128]{3,2,1,0:T(2,128)(2,1)} %copy.67), calls=%async_computation.1 | async-start | bytes 1638400 | tf_op jit(solution)/shard_map/all_to_all | solution.py:191
  212.1 3.1 copy-start.7
  218.8 26.2 %all-to-all-start.2 = ((bf16[10,160,2,128]{3,2,0,1:T(2,128)(2,1)}), bf16[10,160,2,128]{3,2,0,1:T(2,128)(2,1)}, u32[]{:S(2)}, u32[]{:S(2)}) async-start(bf16[10,160,2,128]{3,2,0,1:T(2,128)(2,1)} %copy.70), calls=%async_computation.2 | async-start | bytes 1638400 | tf_op jit(solution)/shard_map/all_to_all | solution.py:196
  227.6 23.2 %copy-start.6 = (bf16[160,10,160]{2,1,0:T(8,128)(2,1)}, bf16[160,10,160]{2,1,0:T(8,128)(2,1)S(1)}, u32[]{:S(2)}) copy-start(bf16[160,10,160]{2,1,0:T(8,128)(2,1)S(1)} %gather_fusion.1) | copy-start | bytes 1536004
  256.1 27.2 %copy-start.18 = (bf16[160,1,320]{2,0,1:T(8,128)(2,1)S(1)}, bf16[160,1,320]{2,0,1:T(8,128)(2,1)}, u32[]{:S(2)}) copy-start(bf16[160,1,320]{2,0,1:T(8,128)(2,1)} %get-tuple-element.612) | copy-start | bytes 307204
  256.1 27.2 %copy-start.19 = (bf16[160,1,320]{2,0,1:T(8,128)(2,1)S(1)}, bf16[160,1,320]{2,0,1:T(8,128)(2,1)}, u32[]{:S(2)}) copy-start(bf16[160,1,320]{2,0,1:T(8,128)(2,1)} %get-tuple-element.613) | copy-start | bytes 307204
  286.3 6.4 copy-start.20
  375.8 24.8 %all-to-all-start.6 = ((bf16[10,160,2,128]{3,2,0,1:T(2,128)(2,1)}), bf16[10,160,2,128]{3,2,0,1:T(2,128)(2,1)}, u32[]{:S(2)}, u32[]{:S(2)}) async-start(bf16[10,160,2,128]{3,2,0,1:T(2,128)(2,1)} %copy.82), calls=%async_computation.6 | async-start | bytes 1638400 | tf_op jit(solution)/shard_map/all_to_all | solution.py:196
  412.1 9.3 %copy-start.21 = (f32[3200]{0:T(1024)S(1)}, f32[3200]{0:T(1024)}, u32[]{:S(2)}) copy-start(f32[3200]{0:T(1024)} %copy-done.20) | copy-start | bytes 38404
  414.7 169.7 %all-to-all-start.7 = ((bf16[10,160,2,128]{3,2,0,1:T(2,128)(2,1)}), bf16[10,160,2,128]{3,2,0,1:T(2,128)(2,1)}, u32[]{:S(2)}, u32[]{:S(2)}) async-start(bf16[10,160,2,128]{3,2,0,1:T(2,128)(2,1)} %copy.85), calls=%async_computation.7 | async-start | bytes 1638400 | tf_op jit(solution)/shard_map/all_to_all | solution.py:205
  421.3 160.8 %all-reduce.4.cloned.1.call-start = ((), (), s32[]{:S(2)}) async-start(), calls=%async_computation.8 | async-start | bytes 1310720 | tf_op jit(solution)/shard_map/psum | solution.py:311
  421.3 4.6 copy-start.2
  430.7 4.9 copy-start.5
  430.7 4.9 copy-start.11
  435.4 402.6 %all-reduce.6.cloned.1.call-start = ((), (), s32[]{:S(2)}) async-start(), calls=%async_computation.9 | async-start | bytes 655360 | tf_op jit(solution)/shard_map/psum | solution.py:312
  440.7 145.4 %copy-start.17 = (bf16[160,1,320]{2,0,1:T(8,128)(2,1)S(1)}, bf16[160,1,320]{2,0,1:T(8,128)(2,1)}, u32[]{:S(2)}) copy-start(bf16[160,1,320]{2,0,1:T(8,128)(2,1)} %copy-done.16) | copy-start | bytes 307204
  589.7 252.8 %copy-start.1 = (bf16[128,256]{1,0:T(8,128)(2,1)S(1)}, bf16[128,256]{1,0:T(8,128)(2,1)}, u32[]{:S(2)}) copy-start(bf16[128,256]{1,0:T(8,128)(2,1)} %param.24) | copy-start | bytes 196612
  (19 other events, 32.3 us)
Sparse Core Ops, SparseCore 0:
  435.5 146.5 all-reduce.3
  589.6 248.3 all-reduce.5
where the time goes:
time: 858 us; the launch traced here: 850 us
  waiting for transfers between devices  362 us (42%)
  blocking collectives  157 us (18%)
  loops' own time  104 us (12%)
  local copies, waits for them, and re-layouts  91.8 us (11%)
  other arithmetic  45.3 us (5%)
  starting transfers between devices  37.8 us (4%)
  matrix products  37.3 us (4%)
  between operations  15 us (2%)
    psum x1, waiting for transfers between devices, shards(): lax.psum((totals[1], totals[2], totals[3], totals[4]), ('dp', 'space'))  167 us
    psum x1, waiting for transfers between devices, shards(): lax.psum(spectral_local.astype(jnp.bfloat16), 'dp').astype(jnp.float32)  141 us
    another operation x1, loops' own time, legendre_tables(): lax.scan(advance, (zeros_start, zeros_start), jnp.arange(LMAX, dtype=jnp....  104 us
    psum x1, blocking collectives, shards(): lax.psum((totals[1], totals[2], totals[3], totals[4]), ('dp', 'space'))  78.9 us
    all_to_all x2, waiting for transfers between devices, from_degrees(): lax.all_to_all(values, 'space', split_axis=1, concat_axis=0, tiled=True)  35.5 us
    all_to_all x1, blocking collectives, to_rows(): lax.all_to_all(values, 'space', split_axis=1, concat_axis=0, tiled=True)  26.6 us
    all_to_all x1, blocking collectives, to_spectral(): lax.all_to_all(values, 'space', split_axis=0, concat_axis=1, tiled=True)  25.7 us
    all_to_all x1, blocking collectives, to_degrees(): lax.all_to_all(values, 'space', split_axis=0, concat_axis=1, tiled=True)  25.6 us
  transfers between devices with their start and end apart: 7, of which 5 were waited for; matrix products, arithmetic and copies ran while one was open for 9% of the time, Pallas kernels for 0%

commit v1 on v0

v1 whole, which is shorter than its diff:
```python
import functools
import math

import jax
import jax.numpy as jnp
import ml_dtypes
import numpy as np
from jax import lax
from jax.experimental import pallas as pl
from jax.experimental.pallas import tpu as pltpu
from jax.sharding import PartitionSpec as P

ROWS = 160
NLON = 320
CHAN = 128
HIDDEN = 256
FORCE = 8
FIRES = 256
NS = 16
JL = 10
HB = 5
MM = 10
FULL = 200
HALF = 104
EPSILON = 1e-06
MESH = pl.DeviceIdType.MESH
F32 = jnp.float32
BF16 = jnp.bfloat16
ROOT = math.sqrt(2.0 / math.pi)
CUBIC = 0.044715


def constant_tables():
    device = np.arange(NS)
    low = 5 * device[None, :] + np.arange(HB)[:, None]
    orders = np.stack([low, ROWS - 1 - low])
    flat = orders.reshape(-1)
    angle = 2.0 * np.pi * ((flat[:, None] * np.arange(NLON)[None, :]) % NLON) / NLON
    cosine, sine = np.cos(angle), np.sin(angle)
    factor = np.where(flat == 0, 1.0, 2.0)[:, None]
    analysis = np.concatenate([cosine, -sine], axis=0) / NLON
    synthesis = np.concatenate([factor * cosine, -factor * sine], axis=0)
    theta = np.pi * (np.arange(ROWS) + 0.5) / ROWS
    start = np.zeros((NS, 16, 256))
    for d in range(NS):
        for r in range(MM):
            m = float(orders[r // HB, r % HB, d])
            log_start = (
                0.5 * math.log((2.0 * m + 1.0) / (4.0 * math.pi))
                + 0.5 * (math.lgamma(m + 0.5) - math.lgamma(m + 1.0))
                - 0.25 * math.log(math.pi)
            )
            start[d, r, :ROWS] = np.exp(log_start + m * np.log(np.sin(theta)))
    waves = np.zeros((8, 256))
    waves[0, :ROWS] = np.cos(theta)
    waves[1, :ROWS] = 2.0 * np.pi * np.pi / ROWS * np.sin(theta)
    narrow = lambda t: np.ascontiguousarray(t).astype(np.float32).astype(ml_dtypes.bfloat16)
    return (
        narrow(analysis),
        narrow(analysis.T),
        narrow(synthesis),
        narrow(synthesis.T),
        start.astype(np.float32),
        waves.astype(np.float32),
    )


def mm_nn(a, b):
    return lax.dot_general(a, b, (((1,), (0,)), ((), ())), preferred_element_type=F32)


def mm_nt(a, b):
    return lax.dot_general(a, b, (((1,), (1,)), ((), ())), preferred_element_type=F32)


def mm_tn(a, b):
    return lax.dot_general(a, b, (((0,), (0,)), ((), ())), preferred_element_type=F32)


def mm_exact(a, b):
    return lax.dot_general(
        a, b, (((1,), (0,)), ((), ())), preferred_element_type=F32, precision=lax.Precision.HIGHEST
    )


def mean(values):
    return jnp.sum(values, axis=-1, keepdims=True) * (1.0 / CHAN)


def normalize(values):
    centre = values - mean(values)
    scale = lax.rsqrt(mean(centre * centre) + EPSILON)
    return centre * scale, scale


def normalize_grad(unit, scale, grad):
    return scale * (grad - mean(grad) - unit * mean(grad * unit))


def gelu_parts(v):
    square = v * v
    t = jnp.tanh(ROOT * v * (1.0 + CUBIC * square))
    half = 0.5 * (1.0 + t)
    slope = half + 0.5 * v * (1.0 - t * t) * (ROOT * (1.0 + 3.0 * CUBIC * square))
    return v * half, slope


def wide(a, b):
    return jnp.concatenate([a, b], axis=-1)


def loop(count, body, start=0):
    def step(index, carry):
        body(index)
        return carry

    lax.fori_loop(start, count, step, 0)


def rounded(v):
    return v.astype(BF16).astype(F32)


def step_kernel(
    nd,
    x_ref,
    cot_ref,
    cells_row,
    cells_col,
    kinds_row,
    kinds_col,
    heat_row,
    heat_col,
    table_ref,
    weight_ref,
    skip_ref,
    up_ref,
    down_ref,
    ana_ref,
    anat_ref,
    syn_ref,
    synt_ref,
    start_ref,
    waves_ref,
    field_out,
    spectral_out,
    skip_out,
    up_out,
    down_out,
    table_out,
    unit,
    scale,
    normed,
    inner_grad,
    fire_t,
    taken,
    made,
    fsend,
    frecv,
    hsend,
    hrecv,
    extra,
    extra_back,
    t0,
    t1,
    plain,
    weighted,
    mix,
    coef,
    small,
    small_in,
    piece1,
    space_in,
    piece2,
    small_all,
    spec,
    spec_send,
    spec_in,
    spec_piece,
    spec_all,
    tab_mine,
    tab_space,
    tab_sum,
    tab_dp,
    ssem,
    rsem,
    dsend,
    drecv,
):
    me = lax.axis_index("space")
    dp = lax.axis_index("dp")
    pr = 640 // nd
    sr = 2560 // nd

    barrier = pltpu.get_barrier_semaphore()

    def greet_space(o):
        pl.semaphore_signal(barrier, 1, device_id={"space": lax.rem(me + o, NS)}, device_id_type=MESH)

    def greet_dp(o):
        pl.semaphore_signal(barrier, 1, device_id={"dp": lax.rem(dp + o, nd)}, device_id_type=MESH)

    loop(NS, greet_space, 1)
    if nd > 1:
        loop(nd, greet_dp, 1)

    def exchange_copy(send, recv, k, target, slot):
        return pltpu.make_async_remote_copy(
            src_ref=send.at[target],
            dst_ref=recv.at[slot],
            send_sem=ssem.at[k, target],
            recv_sem=rsem.at[k, slot],
            device_id={"space": target},
            device_id_type=MESH,
        )

    def send_blocks(send, recv, k, rows):
        def one(o):
            e = lax.rem(me + o, NS)
            send[e] = made[pl.ds(pl.multiple_of(e * rows, 8), rows), :].astype(BF16)
            exchange_copy(send, recv, k, e, me).start()

        loop(NS, one, 1)
        send[me] = made[pl.ds(pl.multiple_of(me * rows, 8), rows), :].astype(BF16)

    def take_blocks(send, recv, k, rows):
        taken[pl.ds(pl.multiple_of(me * rows, 8), rows), :] = send[me].astype(F32)

        def one(o):
            s = lax.rem(me + NS - o, NS)
            exchange_copy(send, recv, k, s, s).wait_recv()
            taken[pl.ds(pl.multiple_of(s * rows, 8), rows), :] = recv[s].astype(F32)

        def sent(o):
            s = lax.rem(me + o, NS)
            exchange_copy(send, recv, k, s, s).wait_send()

        loop(NS, one, 1)
        loop(NS, sent, 1)

    def spread(axis, count, mine, k, source_of, recv, start):
        def one(o):
            t = lax.rem(mine + o, count)
            slot = mine if start else t
            copy = pltpu.make_async_remote_copy(
                src_ref=source_of(t),
                dst_ref=recv.at[slot],
                send_sem=dsend.at[k, t],
                recv_sem=drecv.at[k, slot],
                device_id={axis: t},
                device_id_type=MESH,
            )
            if start:
                copy.start()
            else:
                copy.wait_recv()
                copy.wait_send()

        if count > 1:
            loop(count, one, 1)

    def total(recv, count):
        value = recv[0].astype(F32)
        for t in range(1, count):
            value = value + recv[t].astype(F32)
        return value

    lanes = lax.broadcasted_iota(jnp.int32, (FIRES, 128), 1)
    heat = jnp.broadcast_to(heat_col[...], (FIRES, 128))
    heat0 = rounded(heat)
    heat1 = rounded(heat - heat0)
    heat2 = heat - heat0 - heat1
    parts = jnp.where(lanes < 8, heat0, jnp.where(lanes < 16, heat1, heat2))
    chosen = (jnp.broadcast_to(kinds_col[...], (FIRES, 128)) == (lanes & 7)) & (lanes < 24)
    heats = jnp.where(chosen, parts, 0.0).astype(BF16)
    table_wide = table_ref[...].astype(F32)
    table3 = jnp.concatenate(
        [table_wide, table_wide, table_wide, jnp.zeros((104, CHAN), F32)], axis=0
    )

    def to_orders(j, table, row):
        spectrum = mm_nn(table[...], row)
        for r in range(2 * MM):
            made[pl.ds(j * (2 * MM) + r, NS, stride=FULL), :] = spectrum[r * NS : (r + 1) * NS]

    def from_orders(j, table):
        pieces = [taken[pl.ds(j * (2 * MM) + r, NS, stride=FULL), :] for r in range(2 * MM)]
        return mm_nn(table[...], jnp.concatenate(pieces, axis=0).astype(BF16))

    def field_row(j):
        base = (me * JL + j) * NLON
        cells = lax.broadcasted_iota(jnp.int32, (NLON, FIRES), 0) + base
        hot = jnp.where(cells == cells_row[...], 1.0, 0.0).astype(BF16)
        added = mm_exact(mm_nn(hot, heats), table3)
        value, factor = normalize(x_ref[j].astype(F32) + added)
        unit[j] = value
        scale[j] = jnp.broadcast_to(factor, (NLON, CHAN))
        narrow = value.astype(BF16)
        normed[j] = narrow
        to_orders(j, ana_ref, narrow)

    loop(JL, field_row)
    pl.semaphore_wait(barrier, (NS - 1) + (nd - 1))
    send_blocks(fsend.at[0], frecv.at[0], 0, FULL)

    row16 = lax.broadcasted_iota(jnp.int32, (16, 128), 0)
    order = jnp.where(row16 >= HB, ROWS - 1 - 5 * me - (row16 - HB), 5 * me + row16).astype(F32)
    order2 = order * order
    cos0 = jnp.broadcast_to(waves_ref[0:1, 0:128], (16, 128))
    cos1 = jnp.broadcast_to(waves_ref[0:1, 128:256], (16, 128))

    def advance(l, carry):
        p0, p1, b0, b1 = carry
        lf = jnp.full((16, 128), l, jnp.int32).astype(F32)
        lower = lf - 1.0
        upward = jnp.sqrt(
            jnp.maximum(4.0 * lf * lf - 1.0, 1.0) / jnp.maximum(lf * lf - order2, 1.0)
        )
        downward = jnp.sqrt(
            jnp.maximum(lower * lower - order2, 0.0) / jnp.maximum(4.0 * lower * lower - 1.0, 1.0)
        )
        first = start_ref[me]
        at_start = lf == order
        above = lf > order
        c0 = jnp.where(
            at_start, first[:, 0:128], jnp.where(above, upward * (cos0 * p0 - downward * b0), 0.0)
        )
        c1 = jnp.where(
            at_start, first[:, 128:256], jnp.where(above, upward * (cos1 * p1 - downward * b1), 0.0)
        )
        upper_half = l // 80
        q = l + upper_half * (ROWS - 1 - 2 * l)
        place = (upper_half * HB + q % HB) * NS + q // HB
        t0[pl.ds(place, 16, stride=ROWS), :] = c0
        t1[pl.ds(place, 16, stride=ROWS), :] = c1
        return (c0, c1, p0, p1)

    blank = start_ref[me][:, 0:128] * 0.0
    lax.fori_loop(0, ROWS, advance, (blank, blank, blank, blank))

    def narrow_tables(r):
        at = pl.ds(pl.multiple_of(r * ROWS, 8), ROWS)
        values = wide(t0[at, :], t1[at, :])
        plain[r] = values.astype(BF16)
        weighted[r] = (values * waves_ref[1:2, :]).astype(BF16)

    loop(MM, narrow_tables)

    def build_mix(g):
        real = weight_ref[2 * g]
        imag = weight_ref[2 * g + 1]
        mix[g, 0:128, 0:128] = real
        mix[g, 0:128, 128:256] = imag
        mix[g, 128:256, 0:128] = -imag
        mix[g, 128:256, 128:256] = real

    loop(2 * HB, build_mix)

    rows32 = lax.broadcasted_iota(jnp.int32, (32, FIRES), 0)
    hr = jnp.broadcast_to(heat_row[...], (32, FIRES))
    hr0 = rounded(hr)
    hr1 = rounded(hr - hr0)
    hr2 = hr - hr0 - hr1
    part = jnp.where(rows32 < 8, hr0, jnp.where(rows32 < 16, hr1, hr2))
    pick = (jnp.broadcast_to(kinds_row[...], (32, FIRES)) == (rows32 & 7)) & (rows32 < 24)
    heats_t = jnp.where(pick, part, 0.0).astype(BF16)

    def fire_columns(j):
        base = (me * JL + j) * NLON
        cells = lax.broadcasted_iota(jnp.int32, (FIRES, NLON), 1) + base
        hot = jnp.where(cells == cells_col[...], 1.0, 0.0).astype(BF16)
        fire_t[j] = mm_nn(heats_t, hot)

    loop(JL, fire_columns)

    def analyse(fk, k_in, hk, k_out, table):
        take_blocks(fsend.at[fk], frecv.at[fk], k_in, FULL)

        def field_of(r):
            a = taken[pl.ds(r, ROWS, stride=2 * MM), :]
            b = taken[pl.ds(MM + r, ROWS, stride=2 * MM), :]
            return wide(a, b).astype(BF16)

        def one(i):
            low = mm_nn(table[i][:, 0:ROWS], field_of(i))
            high = mm_nn(table[HB + i][:, 0:ROWS], field_of(HB + i))
            for p in range(2):
                lane = slice(p * 128, (p + 1) * 128)
                for ii in range(HB):
                    ll = low[ii * NS : (ii + 1) * NS, lane]
                    lh = low[(HB + ii) * NS : (HB + ii + 1) * NS, lane]
                    hh = high[(HB + ii) * NS : (HB + ii + 1) * NS, lane]
                    at = p * 50 + i * HB + ii
                    made[pl.ds(at, NS, stride=HALF), :] = lh
                    made[pl.ds(at + 25, NS, stride=HALF), :] = jnp.where(row16 >= me, ll, hh)
                    extra[pl.ds(p * 32 + i * HB + ii, NS, stride=64), :] = rounded(hh)

        loop(HB, one)
        send_blocks(hsend.at[hk], hrecv.at[hk], k_out, HALF)

    row80 = lax.broadcasted_iota(jnp.int32, (80, 256), 0) & 15
    from_low = row80 <= me

    def mix_degrees(hk_in, k_in, hk_out, k_out, backward):
        take_blocks(hsend.at[hk_in], hrecv.at[hk_in], k_in, HALF)
        product = mm_nt if backward else mm_nn
        for ii in range(HB):

            def gather(slot):
                pieces = []
                for i in range(HB):
                    at = slot * 25 + i * HB + ii
                    pieces.append(
                        wide(
                            taken[pl.ds(at, NS, stride=HALF), :],
                            taken[pl.ds(50 + at, NS, stride=HALF), :],
                        )
                    )
                return jnp.concatenate(pieces, axis=0)

            own = wide(
                extra[pl.ds(me * 64 + ii, 8, stride=HB), :],
                extra[pl.ds(me * 64 + 32 + ii, 8, stride=HB), :],
            )
            own = jnp.where(lax.broadcasted_iota(jnp.int32, (8, 256), 0) < HB, own, 0.0)
            second = gather(1)
            rows = jnp.concatenate(
                [gather(0), second, own, jnp.zeros((8, 256), F32)], axis=0
            )
            narrow = rows.astype(BF16)
            second_narrow = second.astype(BF16)
            high = product(narrow, mix[HB + ii])
            low = product(second_narrow, mix[ii])
            mixed_second = jnp.where(from_low, low, high[80:160])
            for p in range(2):
                lane = slice(p * 128, (p + 1) * 128)
                for i in range(HB):
                    at = p * 50 + ii * HB + i
                    made[pl.ds(at, NS, stride=HALF), :] = high[i * NS : (i + 1) * NS, lane]
                    made[pl.ds(at + 25, NS, stride=HALF), :] = mixed_second[
                        i * NS : (i + 1) * NS, lane
                    ]
                extra_back[p * 32 + ii * HB : p * 32 + ii * HB + 8, :] = rounded(high[160:168, lane])
            if backward:
                kept = coef[ii].astype(F32)
                kept_second = kept[80:160]
                kept_high = jnp.concatenate(
                    [kept[0:80], jnp.where(from_low, 0.0, kept_second), kept[160:176]], axis=0
                )
                kept_low = jnp.where(from_low, kept_second, 0.0)
                grad_high = mm_tn(kept_high.astype(BF16), narrow)
                grad_low = mm_tn(kept_low.astype(BF16), second_narrow)
                for half, grad in ((0, grad_low), (1, grad_high)):
                    at = (half * HB + ii) * 256
                    spec[at : at + 128, :] = grad[0:128, 0:128] + grad[128:256, 128:256]
                    spec[at + 128 : at + 256, :] = grad[0:128, 128:256] - grad[128:256, 0:128]
            else:
                coef[ii] = narrow
        send_blocks(hsend.at[hk_out], hrecv.at[hk_out], k_out, HALF)

    def synthesise(hk, k_in, fk, k_out, table):
        take_blocks(hsend.at[hk], hrecv.at[hk], k_in, HALF)

        def one(i):
            def rows_of(slot, ii):
                at = slot * 25 + ii * HB + i
                return wide(
                    taken[pl.ds(at, NS, stride=HALF), :], taken[pl.ds(50 + at, NS, stride=HALF), :]
                )

            seconds = [rows_of(1, ii) for ii in range(HB)]
            firsts = [rows_of(0, ii) for ii in range(HB)]
            mine = lax.broadcasted_iota(jnp.int32, (NS, 256), 0) == me
            highs = []
            for ii in range(HB):
                own = wide(
                    extra_back[pl.ds(ii * HB + i, 1), :], extra_back[pl.ds(32 + ii * HB + i, 1), :]
                )
                highs.append(jnp.where(mine, jnp.broadcast_to(own, (NS, 256)), seconds[ii]))
            low = mm_tn(
                table[i][:, 0:ROWS], jnp.concatenate(seconds + firsts, axis=0).astype(BF16)
            )
            high = mm_tn(
                table[HB + i][:, 0:ROWS], jnp.concatenate(seconds + highs, axis=0).astype(BF16)
            )
            made[pl.ds(i, ROWS, stride=2 * MM), :] = low[:, 0:128]
            made[pl.ds(MM + i, ROWS, stride=2 * MM), :] = low[:, 128:256]
            made[pl.ds(HB + i, ROWS, stride=2 * MM), :] = high[:, 0:128]
            made[pl.ds(MM + HB + i, ROWS, stride=2 * MM), :] = high[:, 128:256]

        loop(HB, one)
        send_blocks(fsend.at[fk], frecv.at[fk], k_out, FULL)

    analyse(0, 0, 0, 1, weighted)
    mix_degrees(0, 1, 1, 2, False)
    synthesise(1, 2, 1, 3, plain)

    take_blocks(fsend.at[1], frecv.at[1], 3, FULL)
    small[...] = jnp.zeros((640, CHAN), F32)

    def middle_row(j):
        row = normed[j]
        inner = from_orders(j, synt_ref) + mm_nn(row, skip_ref[...])
        activated, inner_slope = gelu_parts(inner)
        second, factor = normalize(activated)
        narrow = second.astype(BF16)
        upper = mm_nn(narrow, up_ref[...])
        hidden, slope = gelu_parts(upper)
        incoming = cot_ref[j]
        grad_upper = (mm_nt(incoming, down_ref[...]) * slope).astype(BF16)
        grad_second = mm_nt(grad_upper, up_ref[...])
        small[384:640, :] += mm_tn(hidden.astype(BF16), incoming)
        grad_up = mm_tn(narrow, grad_upper)
        small[128:256, :] += grad_up[:, 0:128]
        small[256:384, :] += grad_up[:, 128:256]
        grad_inner = (normalize_grad(second, factor, grad_second) * inner_slope).astype(BF16)
        small[0:128, :] += mm_tn(row, grad_inner)
        inner_grad[j] = grad_inner
        to_orders(j, syn_ref, grad_inner)

    loop(JL, middle_row)
    send_blocks(fsend.at[2], frecv.at[2], 4, FULL)

    def small_source(t):
        return small.at[pl.ds(pl.multiple_of(t * pr, 8), pr), :]

    spread("dp", nd, dp, 0, small_source, small_in, True)
    small_in[dp] = small[pl.ds(pl.multiple_of(dp * pr, 8), pr), :]

    analyse(2, 4, 2, 5, plain)

    spread("dp", nd, dp, 0, small_source, small_in, False)
    piece1[...] = total(small_in, nd)
    spread("space", NS, me, 1, lambda t: piece1, space_in, True)
    space_in[me] = piece1[...]

    mix_degrees(2, 5, 3, 6, True)

    spread("space", NS, me, 1, lambda t: piece1, space_in, False)
    piece2[...] = total(space_in, NS)
    spread("dp", nd, dp, 2, lambda t: piece2, small_all, True)
    small_all[dp] = piece2[...]

    def narrow_spec(t):
        spec_send[t] = spec[pl.ds(pl.multiple_of(t * sr, 16), sr), :].astype(BF16)

    loop(nd, narrow_spec)
    spread("dp", nd, dp, 3, lambda t: spec_send.at[t], spec_in, True)
    spec_in[dp] = spec_send[dp]

    synthesise(3, 6, 3, 7, weighted)

    spread("dp", nd, dp, 3, lambda t: spec_send.at[t], spec_in, False)
    spec_piece[...] = total(spec_in, nd).astype(BF16)
    spread("dp", nd, dp, 4, lambda t: spec_piece, spec_all, True)
    spec_all[dp] = spec_piece[...]

    take_blocks(fsend.at[3], frecv.at[3], 7, FULL)
    tab_mine[...] = jnp.zeros((32, CHAN), F32)

    def last_row(j):
        grad_normed = from_orders(j, anat_ref) + mm_nt(inner_grad[j], skip_ref[...])
        grad = cot_ref[j].astype(F32) + normalize_grad(unit[j], scale[j], grad_normed)
        field_out[j] = grad.astype(BF16)
        tab_mine[...] += mm_exact(fire_t[j], grad)

    loop(JL, last_row)
    tab_mine[0:8, :] = tab_mine[0:8, :] + tab_mine[8:16, :] + tab_mine[16:24, :]
    spread("space", NS, me, 5, lambda t: tab_mine.at[0:8], tab_space, True)
    tab_space[me] = tab_mine[0:8, :]

    spread("dp", nd, dp, 2, lambda t: piece2, small_all, False)
    flat_small = [small_all[t] for t in range(nd)]
    flat_small = jnp.concatenate(flat_small, axis=0)
    skip_out[...] = flat_small[0:128]
    up_out[:, 0:128] = flat_small[128:256]
    up_out[:, 128:256] = flat_small[256:384]
    down_out[...] = flat_small[384:640]
    spread("dp", nd, dp, 4, lambda t: spec_piece, spec_all, False)

    def widen_spec(t):
        spectral_out[pl.ds(pl.multiple_of(t * sr, 16), sr), :] = spec_all[t].astype(F32)

    loop(nd, widen_spec)

    spread("space", NS, me, 5, lambda t: tab_mine.at[0:8], tab_space, False)
    tab_sum[...] = total(tab_space, NS)
    spread("dp", nd, dp, 6, lambda t: tab_sum, tab_dp, True)
    tab_dp[dp] = tab_sum[...]
    spread("dp", nd, dp, 6, lambda t: tab_sum, tab_dp, False)
    table_out[...] = total(tab_dp, nd)


def shards(
    nd,
    state_field,
    cotangent,
    fire_cells,
    fire_kinds,
    fire_heat,
    forcing_table,
    spectral_weight,
    skip_weight,
    up_weight,
    down_weight,
):
    ana, anat, syn, synt, start, waves = (jnp.asarray(t) for t in constant_tables())
    pr, sr = 640 // nd, 2560 // nd
    operands = (
        state_field[0],
        cotangent[0],
        fire_cells,
        fire_cells.reshape(FIRES, 1),
        fire_kinds,
        fire_kinds.reshape(FIRES, 1),
        fire_heat,
        fire_heat.reshape(FIRES, 1),
        forcing_table,
        spectral_weight.reshape(4 * HB, CHAN, CHAN),
        skip_weight,
        up_weight,
        down_weight,
        ana,
        anat,
        syn,
        synt,
        start,
        waves,
    )
    vmem = pl.BlockSpec(memory_space=pltpu.VMEM)
    out_shape = (
        jax.ShapeDtypeStruct((JL, NLON, CHAN), BF16),
        jax.ShapeDtypeStruct((2560, CHAN), F32),
        jax.ShapeDtypeStruct((CHAN, CHAN), F32),
        jax.ShapeDtypeStruct((CHAN, HIDDEN), F32),
        jax.ShapeDtypeStruct((HIDDEN, CHAN), F32),
        jax.ShapeDtypeStruct((FORCE, CHAN), F32),
    )
    scratch = [
        pltpu.VMEM((JL, NLON, CHAN), F32),
        pltpu.VMEM((JL, NLON, CHAN), F32),
        pltpu.VMEM((JL, NLON, CHAN), BF16),
        pltpu.VMEM((JL, NLON, CHAN), BF16),
        pltpu.VMEM((JL, 32, NLON), F32),
        pltpu.VMEM((NS * FULL, CHAN), F32),
        pltpu.VMEM((NS * FULL, CHAN), F32),
        pltpu.VMEM((4, NS, FULL, CHAN), BF16),
        pltpu.VMEM((4, NS, FULL, CHAN), BF16),
        pltpu.VMEM((4, NS, HALF, CHAN), BF16),
        pltpu.VMEM((4, NS, HALF, CHAN), BF16),
        pltpu.VMEM((NS * 64 + 16, CHAN), F32),
        pltpu.VMEM((72, CHAN), F32),
        pltpu.VMEM((16 * ROWS, 128), F32),
        pltpu.VMEM((16 * ROWS, 128), F32),
        pltpu.VMEM((MM, ROWS, 256), BF16),
        pltpu.VMEM((MM, ROWS, 256), BF16),
        pltpu.VMEM((2 * HB, 256, 256), BF16),
        pltpu.VMEM((HB, 176, 256), BF16),
        pltpu.VMEM((640, CHAN), F32),
        pltpu.VMEM((nd, pr, CHAN), F32),
        pltpu.VMEM((pr, CHAN), F32),
        pltpu.VMEM((NS, pr, CHAN), F32),
        pltpu.VMEM((pr, CHAN), F32),
        pltpu.VMEM((nd, pr, CHAN), F32),
        pltpu.VMEM((2560, CHAN), F32),
        pltpu.VMEM((nd, sr, CHAN), BF16),
        pltpu.VMEM((nd, sr, CHAN), BF16),
        pltpu.VMEM((sr, CHAN), BF16),
        pltpu.VMEM((nd, sr, CHAN), BF16),
        pltpu.VMEM((32, CHAN), F32),
        pltpu.VMEM((NS, FORCE, CHAN), F32),
        pltpu.VMEM((FORCE, CHAN), F32),
        pltpu.VMEM((nd, FORCE, CHAN), F32),
        pltpu.SemaphoreType.DMA((8, NS)),
        pltpu.SemaphoreType.DMA((8, NS)),
        pltpu.SemaphoreType.DMA((7, NS)),
        pltpu.SemaphoreType.DMA((7, NS)),
    ]
    field, spectral, skip, up, down, table = pl.pallas_call(
        functools.partial(step_kernel, nd),
        out_shape=out_shape,
        in_specs=[vmem] * len(operands),
        out_specs=(vmem,) * len(out_shape),
        scratch_shapes=scratch,
        compiler_params=pltpu.CompilerParams(
            collective_id=0, has_side_effects=True, vmem_limit_bytes=60 << 20
        ),
        name="step",
    )(*operands)
    return (field[None], spectral.reshape(spectral_weight.shape), skip, up, down, table)


def solution(mesh):
    return jax.shard_map(
        functools.partial(shards, mesh.shape["dp"]),
        mesh=mesh,
        in_specs=(
            P("dp", "space", None, None),
            P("dp", "space", None, None),
            P("dp", None),
            P("dp", None),
            P("dp", None),
            P(),
            P(None, "space", None, None, None),
            P(),
            P(),
            P(),
        ),
        out_specs=(
            P("dp", "space", None, None),
            P(None, "space", None, None, None),
            P(),
            P(),
            P(),
            P(),
        ),
        check_vma=False,
    )
```

time: 858 us -> 202 us (0.24)
  waiting for transfers between devices: 362 us -> 0 us
  Pallas kernels: 0 us -> 191 us
  blocking collectives: 157 us -> 0 us
  loops' own time: 104 us -> 0 us
  local copies, waits for them, and re-layouts: 91.8 us -> 10.2 us
  other arithmetic: 45.3 us -> 0 us
  starting transfers between devices: 37.8 us -> 0 us
  matrix products: 37.3 us -> 0 us
  between operations: 15 us -> 0.67 us
    psum x2 -> x0, waiting for transfers between devices: 308 us -> none  [the longest x1 167 us: shards(): lax.psum((totals[1], totals[2], totals[3], totals[4]), ('dp', 'space'))]
    pallas_call x0 -> x1, Pallas kernels: none -> 191 us  [shards(): pl.pallas_call(functools.partial(step_kernel, nd), out_shape=out_shape, i...]
    another operation x1 -> x0, loops' own time: 104 us -> none  [legendre_tables(): lax.scan(advance, (zeros_start, zeros_start), jnp.arange(LMAX, dtype=jnp....]
    psum x1 -> x0, blocking collectives: 78.9 us -> none  [shards(): lax.psum((totals[1], totals[2], totals[3], totals[4]), ('dp', 'space'))]
    all_to_all x3 -> x0, blocking collectives: 77.8 us -> none  [the longest x1 26.6 us: to_rows(): lax.all_to_all(values, 'space', split_axis=1, concat_axis=0, tiled=True)]
    all_to_all x5 -> x0, waiting for transfers between devices: 53.3 us -> none  [the longest x2 35.5 us: from_degrees(): lax.all_to_all(values, 'space', split_axis=1, concat_axis=0, tiled=True)]
    all_to_all x5 -> x0, starting transfers between devices: 37.6 us -> none  [the longest x2 12.7 us: from_degrees(): lax.all_to_all(values, 'space', split_axis=1, concat_axis=0, tiled=True)]
    dot_general x21 -> x0, matrix products: 37.3 us -> none  [the longest x2 5.28 us: synthesise_rows(): jnp.einsum('cfg,cft->fgt', legendre, harmonic_coefficients.reshape(degree...]
  transfers between devices with their start and end apart: 7 -> 0, of which waited for: 5 -> 0; matrix products, arithmetic and copies ran while one was open for 9% -> 0% of each run, Pallas kernels for 0% -> 0%
where the time goes in v1:
time: 202 us
  Pallas kernels  191 us (95%)
  local copies, waits for them, and re-layouts  10.2 us (5%)
    pallas_call x1, Pallas kernels, shards(): pl.pallas_call(functools.partial(step_kernel, nd), out_shape=out_shape, i...  191 us
    unnamed x16, local copies, waits for them, and re-layouts  5.81 us

profile of v1, /device:TPU:1, one launch (start us, length us, event | category | flops | bytes accessed | tf_op | source)
XLA Modules:
  0.0 201.8 jit_solution(11454454986316147000)
XLA Ops:
  0.6 1.5 copy.24.heat_col
  2.1 1.5 copy.23.kinds_col
  3.6 1.5 copy.22.cells_col
  5.1 190.9 %step.1 = (bf16[10,320,128]{2,1,0:T(8,128)(2,1)}, f32[2560,128]{1,0:T(8,128)}, f32[128,128]{1,0:T(8,128)}, f32[128,256]{1,0:T(8,128)}, f32[256,128]{1,0:T(8,128)}, /*index=5*/f32[8,128]{1,0:T(8,128)}) custom-call(bf16[10,320,128]{2,1,0:T(8,128)(2,1)} %bitcast.10, bf16[10,320,128]{2,1,0:T(8,128)(2,1)} %bitcast.11, s32[1,256]{1,0:T(1,128)} %cells_row.1, ...), custom_call_target="tpu_custom_call" | custom-call | tf_op jit(solution)/shard_map/step/pallas_call | solution.py:679
  196.0 0.0 copy-start
  196.0 2.2 %copy.31 = bf16[1,10,320,128]{3,2,1,0:T(8,128)(2,1)} copy(bf16[1,10,320,128]{3,2,1,0:T(8,128)(2,1)} %bitcast.9) | data formatting | bytes 1638400
  198.2 0.0 copy-done
  198.2 0.0 copy-start.3
  198.2 0.0 copy-start.2
  198.2 0.0 copy-start.1
  198.2 0.0 copy-start.4
  198.2 1.1 copy.32
  199.3 0.0 copy-done.3
  199.3 0.6 copy.33
  199.9 0.0 copy-done.2
  199.9 0.7 copy.34
  200.6 0.0 copy-done.1
  200.6 0.7 copy.35
  201.2 0.0 copy-done.4
  201.2 0.6 copy.36
Async XLA Ops:
  196.0 2.2 %copy-start = (f32[2560,128]{1,0:T(8,128)S(1)}, f32[2560,128]{1,0:T(8,128)}, u32[]{:S(2)}) copy-start(f32[2560,128]{1,0:T(8,128)} %get-tuple-element.13) | copy-start | bytes 3932164
  198.2 1.1 copy-start.3
  198.2 1.7 copy-start.2
  198.2 2.4 %copy-start.1 = (f32[256,128]{1,0:T(8,128)S(1)}, f32[256,128]{1,0:T(8,128)}, u32[]{:S(2)}) copy-start(f32[256,128]{1,0:T(8,128)} %get-tuple-element.28) | copy-start | bytes 393220
  198.2 3.0 %copy-start.4 = (f32[8,128]{1,0:T(8,128)S(1)}, f32[8,128]{1,0:T(8,128)}, u32[]{:S(2)}) copy-start(f32[8,128]{1,0:T(8,128)} %get-tuple-element.29) | copy-start | bytes 12292

commit v2 on v1

v2 whole, which is shorter than its diff:
```python
import functools
import math

import jax
import jax.numpy as jnp
import ml_dtypes
import numpy as np
from jax import lax
from jax.experimental import pallas as pl
from jax.experimental.pallas import tpu as pltpu
from jax.sharding import PartitionSpec as P

ROWS = 160
NLON = 320
CHAN = 128
HIDDEN = 256
FORCE = 8
FIRES = 256
NS = 16
JL = 10
HB = 5
MM = 10
FULL = 200
PAIR = 40
PARTS = ((0, 2, 40), (2, 3, 64))
OWNERS = 5
EPSILON = 1e-06
MESH = pl.DeviceIdType.MESH
F32 = jnp.float32
BF16 = jnp.bfloat16
ROOT = math.sqrt(2.0 / math.pi)
CUBIC = 0.044715


def constant_tables():
    device = np.arange(NS)
    low = 5 * device[None, :] + np.arange(HB)[:, None]
    orders = np.stack([low, ROWS - 1 - low])
    flat = orders.reshape(-1)
    angle = 2.0 * np.pi * ((flat[:, None] * np.arange(NLON)[None, :]) % NLON) / NLON
    cosine, sine = np.cos(angle), np.sin(angle)
    factor = np.where(flat == 0, 1.0, 2.0)[:, None]
    analysis = np.concatenate([cosine, -sine], axis=0) / NLON
    synthesis = np.concatenate([factor * cosine, -factor * sine], axis=0)
    theta = np.pi * (np.arange(ROWS) + 0.5) / ROWS
    start = np.zeros((NS, 16, 256))
    for d in range(NS):
        for r in range(MM):
            m = float(orders[r // HB, r % HB, d])
            log_start = (
                0.5 * math.log((2.0 * m + 1.0) / (4.0 * math.pi))
                + 0.5 * (math.lgamma(m + 0.5) - math.lgamma(m + 1.0))
                - 0.25 * math.log(math.pi)
            )
            start[d, r, :ROWS] = np.exp(log_start + m * np.log(np.sin(theta)))
    waves = np.zeros((8, 256))
    waves[0, :ROWS] = np.cos(theta)
    waves[1, :ROWS] = 2.0 * np.pi * np.pi / ROWS * np.sin(theta)
    narrow = lambda t: np.ascontiguousarray(t).astype(np.float32).astype(ml_dtypes.bfloat16)
    return (
        narrow(analysis),
        narrow(analysis.T),
        narrow(synthesis),
        narrow(synthesis.T),
        start.astype(np.float32),
        waves.astype(np.float32),
    )


def mm_nn(a, b):
    return lax.dot_general(a, b, (((1,), (0,)), ((), ())), preferred_element_type=F32)


def mm_nt(a, b):
    return lax.dot_general(a, b, (((1,), (1,)), ((), ())), preferred_element_type=F32)


def mm_tn(a, b):
    return lax.dot_general(a, b, (((0,), (0,)), ((), ())), preferred_element_type=F32)


def mm_exact(a, b):
    return lax.dot_general(
        a, b, (((1,), (0,)), ((), ())), preferred_element_type=F32, precision=lax.Precision.HIGHEST
    )


def mean(values):
    return jnp.sum(values, axis=-1, keepdims=True) * (1.0 / CHAN)


def normalize(values):
    centre = values - mean(values)
    scale = lax.rsqrt(mean(centre * centre) + EPSILON)
    return centre * scale, scale


def normalize_grad(unit, scale, grad):
    return scale * (grad - mean(grad) - unit * mean(grad * unit))


def gelu_parts(v):
    square = v * v
    t = jnp.tanh(ROOT * v * (1.0 + CUBIC * square))
    half = 0.5 * (1.0 + t)
    slope = half + 0.5 * v * (1.0 - t * t) * (ROOT * (1.0 + 3.0 * CUBIC * square))
    return v * half, slope


def wide(a, b):
    return jnp.concatenate([a, b], axis=-1)


def loop(count, body, start=0):
    def step(index, carry):
        body(index)
        return carry

    lax.fori_loop(start, count, step, 0)


def rounded(v):
    return v.astype(BF16).astype(F32)


def step_kernel(
    nd,
    x_ref,
    cot_ref,
    cells_row,
    kinds_row,
    heat_row,
    table_ref,
    weight_ref,
    skip_ref,
    up_ref,
    down_ref,
    ana_ref,
    anat_ref,
    syn_ref,
    synt_ref,
    start_ref,
    waves_ref,
    field_out,
    spectral_out,
    skip_out,
    up_out,
    down_out,
    table_out,
    unit,
    scale,
    normed,
    inner_grad,
    fire_g,
    fire_t,
    taken,
    made,
    fsend,
    frecv,
    hsend_a,
    hrecv_a,
    hsend_b,
    hrecv_b,
    extra,
    back_a,
    back_b,
    t0,
    t1,
    plain,
    weighted,
    mix,
    coef_a,
    coef_b,
    grad_a,
    grad_b,
    small,
    small_in,
    piece1,
    own_in,
    own_sum,
    piece2,
    small_all,
    spec,
    spec_send,
    spec_in,
    spec_piece,
    spec_all,
    tab_mine,
    tab_space,
    tab_sum,
    tab_dp,
    ssem,
    rsem,
    dsend,
    drecv,
):
    me = lax.axis_index("space")
    dp = lax.axis_index("dp")
    pr = 640 // nd
    sr = 2560 // nd
    og = pr // OWNERS
    hsend, hrecv = (hsend_a, hsend_b), (hrecv_a, hrecv_b)
    back, coef, grad_rows = (back_a, back_b), (coef_a, coef_b), (grad_a, grad_b)

    barrier = pltpu.get_barrier_semaphore()

    def greet_space(o):
        pl.semaphore_signal(barrier, 1, device_id={"space": lax.rem(me + o, NS)}, device_id_type=MESH)

    def greet_dp(o):
        pl.semaphore_signal(barrier, 1, device_id={"dp": lax.rem(dp + o, nd)}, device_id_type=MESH)

    loop(NS, greet_space, 1)
    if nd > 1:
        loop(nd, greet_dp, 1)

    def exchange(send, recv, at, k, source):
        count = at.size

        def one(o):
            e = lax.rem(me + o, NS)
            send[e, at, :] = made[pl.ds(pl.multiple_of(source(e), 8), count), :].astype(BF16)
            pltpu.make_async_remote_copy(
                src_ref=send.at[e, at],
                dst_ref=recv.at[me, at],
                send_sem=ssem.at[k],
                recv_sem=rsem.at[k],
                device_id={"space": e},
                device_id_type=MESH,
            ).start()

        loop(NS, one, 1)
        recv[me, at, :] = made[pl.ds(pl.multiple_of(source(me), 8), count), :].astype(BF16)

    def whole(send, recv, at, k):
        return pltpu.make_async_remote_copy(
            src_ref=send.at[pl.ds(0, NS - 1), at],
            dst_ref=recv.at[pl.ds(0, NS - 1), at],
            send_sem=ssem.at[k],
            recv_sem=rsem.at[k],
            device_id={"space": lax.rem(me + 1, NS)},
            device_id_type=MESH,
        )

    def arrived(send, recv, at, k, target):
        whole(send, recv, at, k).wait_recv()

        def one(s):
            taken[pl.ds(pl.multiple_of(target(s), 8), at.size), :] = recv[s, at, :].astype(F32)

        loop(NS, one)

    def spread(axis, count, mine, k, source_of, recv, start):
        if count == 1:
            return
        if not start:
            done = pltpu.make_async_remote_copy(
                src_ref=recv.at[pl.ds(0, count - 1)],
                dst_ref=recv.at[pl.ds(0, count - 1)],
                send_sem=dsend.at[k],
                recv_sem=drecv.at[k],
                device_id={axis: lax.rem(mine + 1, count)},
                device_id_type=MESH,
            )
            done.wait_recv()
            done.wait_send()
            return

        def one(o):
            t = lax.rem(mine + o, count)
            pltpu.make_async_remote_copy(
                src_ref=source_of(t),
                dst_ref=recv.at[mine],
                send_sem=dsend.at[k],
                recv_sem=drecv.at[k],
                device_id={axis: t},
                device_id_type=MESH,
            ).start()

        loop(count, one, 1)

    def total(recv, count):
        value = recv[0].astype(F32)
        for t in range(1, count):
            value = value + recv[t].astype(F32)
        return value

    def column(row):
        return jnp.broadcast_to(row.astype(F32), (128, FIRES)).T

    lanes = lax.broadcasted_iota(jnp.int32, (FIRES, 128), 1)
    heat = column(heat_row[...])
    heat0 = rounded(heat)
    heat1 = rounded(heat - heat0)
    heat2 = heat - heat0 - heat1
    parts = jnp.where(lanes < 8, heat0, jnp.where(lanes < 16, heat1, heat2))
    chosen = (column(kinds_row[...]) == (lanes & 7).astype(F32)) & (lanes < 24)
    heats = jnp.where(chosen, parts, 0.0).astype(BF16)
    table_wide = table_ref[...].astype(F32)
    table3 = jnp.concatenate(
        [table_wide, table_wide, table_wide, jnp.zeros((104, CHAN), F32)], axis=0
    )

    def field_row(j):
        base = (me * JL + j) * NLON
        cells = lax.broadcasted_iota(jnp.int32, (NLON, FIRES), 0) + base
        hot = jnp.where(cells == cells_row[...], 1.0, 0.0).astype(BF16)
        fires = mm_nn(hot, heats)
        fire_g[j] = fires
        value, factor = normalize(x_ref[j].astype(F32) + mm_exact(fires, table3))
        unit[j] = value
        scale[j] = jnp.broadcast_to(factor, (NLON, CHAN))
        narrow = value.astype(BF16)
        normed[j] = narrow
        spectrum = mm_nn(ana_ref[...], narrow)
        for p in range(2):
            for h in range(2):
                for i in range(HB):
                    r = (p * MM + h * HB + i) * NS
                    made[pl.ds(i * PAIR + j * 4 + p * 2 + h, NS, stride=FULL), :] = spectrum[r : r + NS]

    loop(JL, field_row)
    pl.semaphore_wait(barrier, (NS - 1) + (nd - 1))
    first_at = [pl.ds(first * PAIR, count * PAIR) for first, count, _ in PARTS]
    for c, at in enumerate(first_at):
        exchange(fsend.at[0], frecv.at[0], at, c, lambda e: e * FULL + at.start)

    row16 = lax.broadcasted_iota(jnp.int32, (16, 128), 0)
    order = jnp.where(row16 >= HB, ROWS - 1 - 5 * me - (row16 - HB), 5 * me + row16).astype(F32)
    order2 = order * order
    cos0 = jnp.broadcast_to(waves_ref[0:1, 0:128], (16, 128))
    cos1 = jnp.broadcast_to(waves_ref[0:1, 128:256], (16, 128))

    def advance(l, carry):
        p0, p1, b0, b1 = carry
        lf = jnp.full((16, 128), l, jnp.int32).astype(F32)
        lower = lf - 1.0
        upward = jnp.sqrt(
            jnp.maximum(4.0 * lf * lf - 1.0, 1.0) / jnp.maximum(lf * lf - order2, 1.0)
        )
        downward = jnp.sqrt(
            jnp.maximum(lower * lower - order2, 0.0) / jnp.maximum(4.0 * lower * lower - 1.0, 1.0)
        )
        first = start_ref[me]
        at_start = lf == order
        above = lf > order
        c0 = jnp.where(
            at_start, first[:, 0:128], jnp.where(above, upward * (cos0 * p0 - downward * b0), 0.0)
        )
        c1 = jnp.where(
            at_start, first[:, 128:256], jnp.where(above, upward * (cos1 * p1 - downward * b1), 0.0)
        )
        upper_half = l // 80
        q = l + upper_half * (ROWS - 1 - 2 * l)
        place = (upper_half * HB + q % HB) * NS + q // HB
        t0[pl.ds(place, 16, stride=ROWS), :] = c0
        t1[pl.ds(place, 16, stride=ROWS), :] = c1
        return (c0, c1, p0, p1)

    blank = start_ref[me][:, 0:128] * 0.0
    lax.fori_loop(0, ROWS, advance, (blank, blank, blank, blank))

    def narrow_tables(r):
        at = pl.ds(pl.multiple_of(r * ROWS, 8), ROWS)
        values = wide(t0[at, :], t1[at, :])
        plain[r] = values.astype(BF16)
        weighted[r] = (values * waves_ref[1:2, :]).astype(BF16)

    loop(MM, narrow_tables)

    def build_mix(g):
        real = weight_ref[2 * g]
        imag = weight_ref[2 * g + 1]
        mix[g, 0:128, 0:128] = real
        mix[g, 0:128, 128:256] = imag
        mix[g, 128:256, 0:128] = -imag
        mix[g, 128:256, 128:256] = real

    loop(2 * HB, build_mix)

    def fire_columns(j):
        fire_t[j] = fire_g[j].T[0:32]

    loop(JL, fire_columns)

    def analyse(c, k, hk, table, rows_of):
        first, count, height = PARTS[c]

        def one(i):
            low = mm_nn(table[i][:, 0:ROWS], rows_of(0, i))
            high = mm_nn(table[HB + i][:, 0:ROWS], rows_of(1, i))
            for p in range(2):
                lane = slice(p * 128, (p + 1) * 128)
                for ii in range(HB):
                    ll = low[ii * NS : (ii + 1) * NS, lane]
                    lh = low[(HB + ii) * NS : (HB + ii + 1) * NS, lane]
                    hh = high[(HB + ii) * NS : (HB + ii + 1) * NS, lane]
                    at = p * 10 * count + ii * count + i - first
                    made[pl.ds(at, NS, stride=height), :] = lh
                    made[pl.ds(at + 5 * count, NS, stride=height), :] = jnp.where(row16 >= me, ll, hh)
                    extra[pl.ds(p * 32 + i * HB + ii, NS, stride=64), :] = rounded(hh)

        loop(first + count, one, first)
        exchange(
            hsend[c].at[hk], hrecv[c].at[hk], pl.ds(0, height), k, lambda e: e * height
        )

    def first_rows(h, i):
        a = taken[pl.ds(i * 640 + h, ROWS, stride=4), :]
        b = taken[pl.ds(i * 640 + 2 + h, ROWS, stride=4), :]
        return wide(a, b).astype(BF16)

    def later_rows(h, i):
        a = taken[pl.ds(h * HB + i, ROWS, stride=2 * MM), :]
        b = taken[pl.ds(MM + h * HB + i, ROWS, stride=2 * MM), :]
        return wide(a, b).astype(BF16)

    def mix_degrees(c, hk_in, k_in, hk_out, k_out, backward):
        first, count, height = PARTS[c]
        n = count * NS
        at = pl.ds(0, height)
        arrived(hsend[c].at[hk_in], hrecv[c].at[hk_in], at, k_in, lambda s: s * height)
        product = mm_nt if backward else mm_nn
        from_low = (lax.broadcasted_iota(jnp.int32, (n, 256), 0) & 15) <= me
        for ii in range(HB):

            def gather(slot):
                pieces = []
                for i in range(count):
                    r = slot * 5 * count + ii * count + i
                    pieces.append(
                        wide(
                            taken[pl.ds(r, NS, stride=height), :],
                            taken[pl.ds(10 * count + r, NS, stride=height), :],
                        )
                    )
                return jnp.concatenate(pieces, axis=0)

            own = wide(
                extra[pl.ds(me * 64 + first * HB + ii, 8, stride=HB), :],
                extra[pl.ds(me * 64 + 32 + first * HB + ii, 8, stride=HB), :],
            )
            own = jnp.where(lax.broadcasted_iota(jnp.int32, (8, 256), 0) < count, own, 0.0)
            second = gather(1)
            rows = jnp.concatenate([gather(0), second, own, jnp.zeros((8, 256), F32)], axis=0)
            narrow = rows.astype(BF16)
            high = product(narrow, mix[HB + ii])
            low = product(second.astype(BF16), mix[ii])
            mixed_second = jnp.where(from_low, low, high[n : 2 * n])
            for p in range(2):
                lane = slice(p * 128, (p + 1) * 128)
                for i in range(count):
                    r = p * 10 * count + ii * count + i
                    piece = slice(i * NS, (i + 1) * NS)
                    made[pl.ds(r, NS, stride=height), :] = high[piece, lane]
                    made[pl.ds(r + 5 * count, NS, stride=height), :] = mixed_second[piece, lane]
                at_own = p * 32 + ii * count
                back[c][at_own : at_own + 8, :] = rounded(high[2 * n : 2 * n + 8, lane])
            if backward:
                grad_rows[c][ii] = narrow
            else:
                coef[c][ii] = narrow
        exchange(hsend[c].at[hk_out], hrecv[c].at[hk_out], at, k_out, lambda e: e * height)

    def weight_gradient(ii):
        grad_low = jnp.zeros((256, 256), F32)
        grad_high = jnp.zeros((256, 256), F32)
        for c, (_, count, _) in enumerate(PARTS):
            n = count * NS
            kept = coef[c][ii].astype(F32)
            others = grad_rows[c][ii]
            from_low = (lax.broadcasted_iota(jnp.int32, (n, 256), 0) & 15) <= me
            second = kept[n : 2 * n]
            kept_high = jnp.concatenate(
                [kept[0:n], jnp.where(from_low, 0.0, second), kept[2 * n : 2 * n + 16]], axis=0
            )
            kept_low = jnp.where(from_low, second, 0.0)
            grad_high = grad_high + mm_tn(kept_high.astype(BF16), others)
            grad_low = grad_low + mm_tn(kept_low.astype(BF16), others[n : 2 * n])
        for half, grad in ((0, grad_low), (1, grad_high)):
            at = pl.multiple_of((half * HB + ii) * 256, 256)
            spec[pl.ds(at, 128), :] = grad[0:128, 0:128] + grad[128:256, 128:256]
            spec[pl.ds(at + 128, 128), :] = grad[0:128, 128:256] - grad[128:256, 0:128]

    def synthesise(c, hk, k_in, table):
        first, count, height = PARTS[c]
        arrived(
            hsend[c].at[hk], hrecv[c].at[hk], pl.ds(0, height), k_in, lambda s: s * height
        )

        def one(i):
            def rows_of(slot, ii):
                r = slot * 5 * count + ii * count + i - first
                return wide(
                    taken[pl.ds(r, NS, stride=height), :],
                    taken[pl.ds(10 * count + r, NS, stride=height), :],
                )

            seconds = [rows_of(1, ii) for ii in range(HB)]
            firsts = [rows_of(0, ii) for ii in range(HB)]
            mine = lax.broadcasted_iota(jnp.int32, (NS, 256), 0) == me
            highs = []
            for ii in range(HB):
                r = ii * count + i - first
                own = wide(back[c][pl.ds(r, 1), :], back[c][pl.ds(32 + r, 1), :])
                highs.append(jnp.where(mine, jnp.broadcast_to(own, (NS, 256)), seconds[ii]))
            low = mm_tn(
                table[i][:, 0:ROWS], jnp.concatenate(seconds + firsts, axis=0).astype(BF16)
            )
            high = mm_tn(
                table[HB + i][:, 0:ROWS], jnp.concatenate(seconds + highs, axis=0).astype(BF16)
            )
            made[pl.ds(i, ROWS, stride=2 * MM), :] = low[:, 0:128]
            made[pl.ds(MM + i, ROWS, stride=2 * MM), :] = low[:, 128:256]
            made[pl.ds(HB + i, ROWS, stride=2 * MM), :] = high[:, 0:128]
            made[pl.ds(MM + HB + i, ROWS, stride=2 * MM), :] = high[:, 128:256]

        loop(first + count, one, first)

    def pair_rows(c):
        return pl.ds(pl.multiple_of(c * PAIR, 8), PAIR)

    def send_pair(fk, k, c):
        exchange(fsend.at[fk], frecv.at[fk], pair_rows(c), k + c, lambda e: e * FULL + c * PAIR)

    def take_pair(fk, k, c):
        arrived(fsend.at[fk], frecv.at[fk], pair_rows(c), k + c, lambda s: s * FULL + c * PAIR)

    def from_orders(j, table):
        pieces = [taken[pl.ds(j * (2 * MM) + r, NS, stride=FULL), :] for r in range(2 * MM)]
        return mm_nn(table[...], jnp.concatenate(pieces, axis=0).astype(BF16))

    for c, (first, count, _) in enumerate(PARTS):
        for i in range(first, first + count):
            at = pl.ds(i * PAIR, PAIR)
            if i == first:
                whole(fsend.at[0], frecv.at[0], first_at[c], c).wait_recv()

            def first_block(s):
                taken[pl.ds(pl.multiple_of(i * 640 + s * PAIR, 8), PAIR), :] = frecv[0, s, at, :].astype(F32)

            loop(NS, first_block)
        analyse(c, 2 + c, 0, weighted, first_rows)
    for c in range(2):
        mix_degrees(c, 0, 2 + c, 1, 4 + c, False)
    for c in range(2):
        synthesise(c, 1, 4 + c, plain)
    loop(HB, lambda c: send_pair(1, 6, c))

    small[...] = jnp.zeros((640, CHAN), F32)

    def middle_row(j):
        row = normed[j]
        inner = from_orders(j, synt_ref) + mm_nn(row, skip_ref[...])
        activated, inner_slope = gelu_parts(inner)
        second, factor = normalize(activated)
        narrow = second.astype(BF16)
        upper = mm_nn(narrow, up_ref[...])
        hidden, slope = gelu_parts(upper)
        incoming = cot_ref[j]
        grad_upper = (mm_nt(incoming, down_ref[...]) * slope).astype(BF16)
        grad_second = mm_nt(grad_upper, up_ref[...])
        small[384:640, :] += mm_tn(hidden.astype(BF16), incoming)
        grad_up = mm_tn(narrow, grad_upper)
        small[128:256, :] += grad_up[:, 0:128]
        small[256:384, :] += grad_up[:, 128:256]
        grad_inner = (normalize_grad(second, factor, grad_second) * inner_slope).astype(BF16)
        small[0:128, :] += mm_tn(row, grad_inner)
        inner_grad[j] = grad_inner
        spectrum = mm_nn(syn_ref[...], grad_inner)
        for r in range(2 * MM):
            made[pl.ds(j * (2 * MM) + r, NS, stride=FULL), :] = spectrum[r * NS : (r + 1) * NS]

    def middle_pair(c):
        take_pair(1, 6, c)
        loop(2, lambda t: middle_row(2 * c + t))
        send_pair(2, 11, c)

    loop(HB, middle_pair)

    def small_source(t):
        return small.at[pl.ds(pl.multiple_of(t * pr, 8), pr), :]

    spread("dp", nd, dp, 0, small_source, small_in, True)
    small_in[dp] = small[pl.ds(pl.multiple_of(dp * pr, 8), pr), :]

    loop(HB, lambda c: take_pair(2, 11, c))
    for c in range(2):
        analyse(c, 16 + c, 2, plain, later_rows)

    spread("dp", nd, dp, 0, small_source, small_in, False)
    piece1[...] = total(small_in, nd)

    def owner_copy(e, slot):
        return pltpu.make_async_remote_copy(
            src_ref=piece1.at[pl.ds(pl.multiple_of(e * og, 8), og)],
            dst_ref=own_in.at[slot],
            send_sem=dsend.at[1],
            recv_sem=drecv.at[1],
            device_id={"space": e},
            device_id_type=MESH,
        )

    def to_owner(e):
        @pl.when(e != me)
        def _():
            owner_copy(e, me).start()

    loop(OWNERS, to_owner)

    for c in range(2):
        mix_degrees(c, 2, 16 + c, 3, 18 + c, True)

    def owner_out(t, slot):
        return pltpu.make_async_remote_copy(
            src_ref=own_sum,
            dst_ref=piece2.at[slot],
            send_sem=dsend.at[2],
            recv_sem=drecv.at[2],
            device_id={"space": t},
            device_id_type=MESH,
        )

    @pl.when(me < OWNERS)
    def _():
        own_in[me] = piece1[pl.ds(pl.multiple_of(me * og, 8), og), :]
        gathered = pltpu.make_async_remote_copy(
            src_ref=own_in.at[pl.ds(0, NS - 1)],
            dst_ref=own_in.at[pl.ds(0, NS - 1)],
            send_sem=dsend.at[1],
            recv_sem=drecv.at[1],
            device_id={"space": lax.rem(me + 1, NS)},
            device_id_type=MESH,
        )
        gathered.wait_recv()
        own_sum[...] = total(own_in, NS)
        piece2[me] = own_sum[...]

        def tell(o):
            owner_out(lax.rem(me + o, NS), me).start()

        loop(NS, tell, 1)

    loop(HB, weight_gradient)

    def narrow_spec(t):
        spec_send[t] = spec[pl.ds(pl.multiple_of(t * sr, 16), sr), :].astype(BF16)

    loop(nd, narrow_spec)
    spread("dp", nd, dp, 3, lambda t: spec_send.at[t], spec_in, True)
    spec_in[dp] = spec_send[dp]

    for c in range(2):
        synthesise(c, 3, 18 + c, weighted)
    loop(HB, lambda c: send_pair(3, 20, c))

    def counted(ref, count, k):
        return pltpu.make_async_remote_copy(
            src_ref=ref.at[pl.ds(0, count)],
            dst_ref=ref.at[pl.ds(0, count)],
            send_sem=dsend.at[k],
            recv_sem=drecv.at[k],
            device_id={"space": lax.rem(me + 1, NS)},
            device_id_type=MESH,
        )

    @pl.when(me < OWNERS)
    def _():
        counted(own_in, OWNERS - 1, 1).wait_send()
        counted(piece2, OWNERS - 1, 2).wait_recv()
        counted(own_in, NS - 1, 2).wait_send()

    @pl.when(me >= OWNERS)
    def _():
        counted(own_in, OWNERS, 1).wait_send()
        counted(piece2, OWNERS, 2).wait_recv()

    spread("dp", nd, dp, 4, lambda t: piece2, small_all, True)
    small_all[dp] = piece2[...]

    spread("dp", nd, dp, 3, lambda t: spec_send.at[t], spec_in, False)
    spec_piece[...] = total(spec_in, nd).astype(BF16)
    spread("dp", nd, dp, 5, lambda t: spec_piece, spec_all, True)
    spec_all[dp] = spec_piece[...]

    for c, at in enumerate(first_at):
        whole(fsend.at[0], frecv.at[0], at, c).wait_send()
    for k, hk in ((2, 0), (4, 1), (16, 2), (18, 3)):
        for c, (_, _, height) in enumerate(PARTS):
            whole(hsend[c].at[hk], hrecv[c].at[hk], pl.ds(0, height), k + c).wait_send()
    for k, fk in ((6, 1), (11, 2)):
        loop(HB, lambda c: whole(fsend.at[fk], frecv.at[fk], pair_rows(c), k + c).wait_send())

    tab_mine[...] = jnp.zeros((32, CHAN), F32)

    def last_row(j):
        grad_normed = from_orders(j, anat_ref) + mm_nt(inner_grad[j], skip_ref[...])
        grad = cot_ref[j].astype(F32) + normalize_grad(unit[j], scale[j], grad_normed)
        field_out[j] = grad.astype(BF16)
        tab_mine[...] += mm_exact(fire_t[j], grad)

    def last_pair(c):
        take_pair(3, 20, c)
        loop(2, lambda t: last_row(2 * c + t))

    loop(HB, last_pair)
    tab_mine[0:8, :] = tab_mine[0:8, :] + tab_mine[8:16, :] + tab_mine[16:24, :]
    spread("space", NS, me, 6, lambda t: tab_mine.at[0:8], tab_space, True)
    tab_space[me] = tab_mine[0:8, :]

    loop(HB, lambda c: whole(fsend.at[3], frecv.at[3], pair_rows(c), 20 + c).wait_send())
    spread("dp", nd, dp, 4, lambda t: piece2, small_all, False)
    flat_small = [small_all[t, g] for t in range(nd) for g in range(OWNERS)]
    flat_small = jnp.concatenate(flat_small, axis=0)
    skip_out[...] = flat_small[0:128]
    up_out[:, 0:128] = flat_small[128:256]
    up_out[:, 128:256] = flat_small[256:384]
    down_out[...] = flat_small[384:640]
    spread("dp", nd, dp, 5, lambda t: spec_piece, spec_all, False)

    def copy_spec(t):
        spectral_out[pl.ds(pl.multiple_of(t * sr, 16), sr), :] = spec_all[t]

    loop(nd, copy_spec)

    spread("space", NS, me, 6, lambda t: tab_mine.at[0:8], tab_space, False)
    tab_sum[...] = total(tab_space, NS)
    spread("dp", nd, dp, 7, lambda t: tab_sum, tab_dp, True)
    tab_dp[dp] = tab_sum[...]
    spread("dp", nd, dp, 7, lambda t: tab_sum, tab_dp, False)
    table_out[...] = total(tab_dp, nd)


def shards(
    nd,
    state_field,
    cotangent,
    fire_cells,
    fire_kinds,
    fire_heat,
    forcing_table,
    spectral_weight,
    skip_weight,
    up_weight,
    down_weight,
):
    ana, anat, syn, synt, start, waves = (jnp.asarray(t) for t in constant_tables())
    pr, sr = 640 // nd, 2560 // nd
    operands = (
        state_field[0],
        cotangent[0],
        fire_cells,
        fire_kinds,
        fire_heat,
        forcing_table,
        spectral_weight.reshape(4 * HB, CHAN, CHAN),
        skip_weight,
        up_weight,
        down_weight,
        ana,
        anat,
        syn,
        synt,
        start,
        waves,
    )
    vmem = pl.BlockSpec(memory_space=pltpu.VMEM)
    out_shape = (
        jax.ShapeDtypeStruct((JL, NLON, CHAN), BF16),
        jax.ShapeDtypeStruct((2560, CHAN), BF16),
        jax.ShapeDtypeStruct((CHAN, CHAN), F32),
        jax.ShapeDtypeStruct((CHAN, HIDDEN), F32),
        jax.ShapeDtypeStruct((HIDDEN, CHAN), F32),
        jax.ShapeDtypeStruct((FORCE, CHAN), F32),
    )
    (_, ca, ha), (_, cb, hb) = PARTS
    scratch = [
        pltpu.VMEM((JL, NLON, CHAN), F32),
        pltpu.VMEM((JL, NLON, CHAN), F32),
        pltpu.VMEM((JL, NLON, CHAN), BF16),
        pltpu.VMEM((JL, NLON, CHAN), BF16),
        pltpu.VMEM((JL, NLON, CHAN), F32),
        pltpu.VMEM((JL, 32, NLON), F32),
        pltpu.VMEM((NS * FULL, CHAN), F32),
        pltpu.VMEM((NS * FULL, CHAN), F32),
        pltpu.VMEM((4, NS, FULL, CHAN), BF16),
        pltpu.VMEM((4, NS, FULL, CHAN), BF16),
        pltpu.VMEM((4, NS, ha, CHAN), BF16),
        pltpu.VMEM((4, NS, ha, CHAN), BF16),
        pltpu.VMEM((4, NS, hb, CHAN), BF16),
        pltpu.VMEM((4, NS, hb, CHAN), BF16),
        pltpu.VMEM((NS * 64 + 32, CHAN), F32),
        pltpu.VMEM((64, CHAN), F32),
        pltpu.VMEM((64, CHAN), F32),
        pltpu.VMEM((16 * ROWS, 128), F32),
        pltpu.VMEM((16 * ROWS, 128), F32),
        pltpu.VMEM((MM, ROWS, 256), BF16),
        pltpu.VMEM((MM, ROWS, 256), BF16),
        pltpu.VMEM((2 * HB, 256, 256), BF16),
        pltpu.VMEM((HB, 2 * NS * ca + 16, 256), BF16),
        pltpu.VMEM((HB, 2 * NS * cb + 16, 256), BF16),
        pltpu.VMEM((HB, 2 * NS * ca + 16, 256), BF16),
        pltpu.VMEM((HB, 2 * NS * cb + 16, 256), BF16),
        pltpu.VMEM((640, CHAN), F32),
        pltpu.VMEM((nd, pr, CHAN), F32),
        pltpu.VMEM((pr, CHAN), F32),
        pltpu.VMEM((NS, pr // OWNERS, CHAN), F32),
        pltpu.VMEM((pr // OWNERS, CHAN), F32),
        pltpu.VMEM((OWNERS, pr // OWNERS, CHAN), F32),
        pltpu.VMEM((nd, OWNERS, pr // OWNERS, CHAN), F32),
        pltpu.VMEM((2560, CHAN), F32),
        pltpu.VMEM((nd, sr, CHAN), BF16),
        pltpu.VMEM((nd, sr, CHAN), BF16),
        pltpu.VMEM((sr, CHAN), BF16),
        pltpu.VMEM((nd, sr, CHAN), BF16),
        pltpu.VMEM((32, CHAN), F32),
        pltpu.VMEM((NS, FORCE, CHAN), F32),
        pltpu.VMEM((FORCE, CHAN), F32),
        pltpu.VMEM((nd, FORCE, CHAN), F32),
        pltpu.SemaphoreType.DMA((25,)),
        pltpu.SemaphoreType.DMA((25,)),
        pltpu.SemaphoreType.DMA((8,)),
        pltpu.SemaphoreType.DMA((8,)),
    ]
    field, spectral, skip, up, down, table = pl.pallas_call(
        functools.partial(step_kernel, nd),
        out_shape=out_shape,
        in_specs=[vmem] * len(operands),
        out_specs=(vmem,) * len(out_shape),
        scratch_shapes=scratch,
        compiler_params=pltpu.CompilerParams(
            collective_id=0, has_side_effects=True, vmem_limit_bytes=60 << 20
        ),
        name="step",
    )(*operands)
    spectral = spectral.reshape(spectral_weight.shape).astype(F32)
    return (field[None], spectral, skip, up, down, table)


def solution(mesh):
    return jax.shard_map(
        functools.partial(shards, mesh.shape["dp"]),
        mesh=mesh,
        in_specs=(
            P("dp", "space", None, None),
            P("dp", "space", None, None),
            P("dp", None),
            P("dp", None),
            P("dp", None),
            P(),
            P(None, "space", None, None, None),
            P(),
            P(),
            P(),
        ),
        out_specs=(
            P("dp", "space", None, None),
            P(None, "space", None, None, None),
            P(),
            P(),
            P(),
            P(),
        ),
        check_vma=False,
    )
```

time: 202 us -> 161 us (0.80)
  Pallas kernels: 191 us -> 155 us
  local copies, waits for them, and re-layouts: 10.2 us -> 3.45 us
  other arithmetic: 0 us -> 2.36 us
    pallas_call x1, Pallas kernels: 191 us -> 155 us  [shards(): pl.pallas_call(functools.partial(step_kernel, nd), out_shape=out_shape, i...]
    reshape x3 -> x0, local copies, waits for them, and re-layouts: 4.42 us -> none  [the longest x1 1.48 us: shards(): fire_heat.reshape(FIRES, 1)]
    unnamed x16 -> x15, local copies, waits for them, and re-layouts: 5.81 us -> 3.45 us
    convert_element_type x0 -> x1, other arithmetic: none -> 2.36 us  [shards(): spectral = spectral.reshape(spectral_weight.shape).astype(F32)]
where the time goes in v2:
time: 161 us
  Pallas kernels  155 us (96%)
  local copies, waits for them, and re-layouts  3.45 us (2%)
  other arithmetic  2.36 us (1%)
    pallas_call x1, Pallas kernels, shards(): pl.pallas_call(functools.partial(step_kernel, nd), out_shape=out_shape, i...  155 us
    unnamed x15, local copies, waits for them, and re-layouts  3.45 us

profile of v2, /device:TPU:1, one launch (start us, length us, event | category | flops | bytes accessed | tf_op | source)
XLA Modules:
  0.0 161.0 jit_solution(10577444540041695286)
XLA Ops:
  0.6 154.5 %step.1 = (bf16[10,320,128]{2,1,0:T(8,128)(2,1)}, bf16[2560,128]{1,0:T(8,128)(2,1)}, f32[128,128]{1,0:T(8,128)}, f32[128,256]{1,0:T(8,128)}, f32[256,128]{1,0:T(8,128)}, /*index=5*/f32[8,128]{1,0:T(8,128)}) custom-call(bf16[10,320,128]{2,1,0:T(8,128)(2,1)} %bitcast.6, bf16[10,320,128]{2,1,0:T(8,128)(2,1)} %bitcast.7, s32[1,256]{1,0:T(1,128)} %cells_row.1, ...), custom_call_target="tpu_custom_call" | custom-call | tf_op jit(solution)/shard_map/step/pallas_call | solution.py:825
  155.2 0.0 copy-start
  155.2 0.0 copy-start.3
  155.2 2.4 %convert.1 = f32[2,5,2,128,128]{4,3,2,1,0:T(8,128)} convert(bf16[2,5,2,128,128]{4,3,2,1,0:T(8,128)(2,1)} %bitcast.10) | non-fusion elementwise | flops 327680 | bytes 1966080 | tf_op jit(solution)/shard_map/convert_element_type | solution.py:836
  157.5 0.0 copy-done
  157.5 0.0 copy-start.2
  157.5 0.0 copy-start.1
  157.5 0.0 copy-start.4
  157.5 0.9 copy.27
  158.4 0.0 copy-done.3
  158.4 0.6 copy.28
  159.1 0.0 copy-done.2
  159.1 0.7 copy.29
  159.7 0.0 copy-done.1
  159.7 0.7 copy.30
  160.4 0.0 copy-done.4
  160.4 0.6 copy.31
Async XLA Ops:
  155.2 2.4 %copy-start = (bf16[10,320,128]{2,1,0:T(8,128)(2,1)S(1)}, bf16[10,320,128]{2,1,0:T(8,128)(2,1)}, u32[]{:S(2)}) copy-start(bf16[10,320,128]{2,1,0:T(8,128)(2,1)} %get-tuple-element.12) | copy-start | bytes 2457604
  155.2 3.3 %copy-start.3 = (f32[128,128]{1,0:T(8,128)S(1)}, f32[128,128]{1,0:T(8,128)}, u32[]{:S(2)}) copy-start(f32[128,128]{1,0:T(8,128)} %get-tuple-element.26) | copy-start | bytes 196612
  157.5 1.5 copy-start.2
  157.5 2.2 %copy-start.1 = (f32[256,128]{1,0:T(8,128)S(1)}, f32[256,128]{1,0:T(8,128)}, u32[]{:S(2)}) copy-start(f32[256,128]{1,0:T(8,128)} %get-tuple-element.28) | copy-start | bytes 393220
  157.5 2.9 %copy-start.4 = (f32[8,128]{1,0:T(8,128)S(1)}, f32[8,128]{1,0:T(8,128)}, u32[]{:S(2)}) copy-start(f32[8,128]{1,0:T(8,128)} %get-tuple-element.29) | copy-start | bytes 12292

commit v3 on v2

--- a/solution.py
+++ b/solution.py
@@ -21,8 +21,9 @@
 HB = 5
 MM = 10
 FULL = 200
-PAIR = 40
 PARTS = ((0, 2, 40), (2, 3, 64))
+ROW_PARTS = ((0, 8), (80, 12))
+OPERANDS = 16
 OWNERS = 5
 EPSILON = 1e-06
 MESH = pl.DeviceIdType.MESH
@@ -123,24 +124,41 @@
     return v.astype(BF16).astype(F32)
 
 
-def step_kernel(
+def step_kernel(nd, *refs):
+    outside, results = refs[:OPERANDS], refs[OPERANDS : OPERANDS + 6]
+    inside, sems = refs[OPERANDS + 6 : 2 * OPERANDS + 6], refs[2 * OPERANDS + 6]
+    copies = [
+        pltpu.make_async_copy(outside[n], inside[n], sems.at[n]) for n in range(OPERANDS)
+    ]
+    for copy in copies:
+        copy.start()
+
+    def ready(first, last):
+        for copy in copies[first:last]:
+            copy.wait()
+
+    step_body(nd, ready, *inside, *results, *refs[2 * OPERANDS + 7 :])
+
+
+def step_body(
     nd,
+    ready,
     x_ref,
-    cot_ref,
     cells_row,
     kinds_row,
     heat_row,
     table_ref,
+    ana_ref,
+    start_ref,
+    waves_ref,
     weight_ref,
+    cot_ref,
+    synt_ref,
     skip_ref,
     up_ref,
     down_ref,
-    ana_ref,
+    syn_ref,
     anat_ref,
-    syn_ref,
-    synt_ref,
-    start_ref,
-    waves_ref,
     field_out,
     spectral_out,
     skip_out,
@@ -182,6 +200,8 @@
     small_all,
     spec,
     spec_send,
+    spec_core,
+    spec_mine,
     spec_in,
     spec_piece,
     spec_all,
@@ -197,7 +217,7 @@
     me = lax.axis_index("space")
     dp = lax.axis_index("dp")
     pr = 640 // nd
-    sr = 2560 // nd
+    sr = 1280 // max(nd // 2, 1)
     og = pr // OWNERS
     hsend, hrecv = (hsend_a, hsend_b), (hrecv_a, hrecv_b)
     back, coef, grad_rows = (back_a, back_b), (coef_a, coef_b), (grad_a, grad_b)
@@ -285,6 +305,8 @@
             value = value + recv[t].astype(F32)
         return value
 
+    ready(0, 6)
+
     def column(row):
         return jnp.broadcast_to(row.astype(F32), (128, FIRES)).T
 
@@ -312,19 +334,51 @@
         scale[j] = jnp.broadcast_to(factor, (NLON, CHAN))
         narrow = value.astype(BF16)
         normed[j] = narrow
-        spectrum = mm_nn(ana_ref[...], narrow)
-        for p in range(2):
-            for h in range(2):
-                for i in range(HB):
-                    r = (p * MM + h * HB + i) * NS
-                    made[pl.ds(i * PAIR + j * 4 + p * 2 + h, NS, stride=FULL), :] = spectrum[r : r + NS]
-
-    loop(JL, field_row)
+        to_orders(j, ana_ref, narrow)
+
+    def to_orders(j, table, row):
+        spectrum = mm_nn(table[...], row)
+        for c, (first, count, _) in enumerate(PARTS):
+            start, width = ROW_PARTS[c]
+            for r in range(width):
+                p, h, i = r // (2 * count), r // count % 2, first + r % count
+                at = (p * MM + h * HB + i) * NS
+                made[pl.ds(start + j * width + r, NS, stride=FULL), :] = spectrum[at : at + NS]
+
+    def rows_at(c, pair=None):
+        start, width = ROW_PARTS[c]
+        if pair is None:
+            return pl.ds(start, JL * width)
+        return pl.ds(pl.multiple_of(start + pair * 2 * width, 8), 2 * width)
+
+    def send_rows(fk, k, c, pair=None):
+        at = rows_at(c, pair)
+        exchange(fsend.at[fk], frecv.at[fk], at, k, lambda e: e * FULL + at.start)
+
+    def rows_arrived(fk, k, c, pair=None):
+        at = rows_at(c, pair)
+        start, width = ROW_PARTS[c]
+        skip = NS * start - start
+        arrived(
+            fsend.at[fk], frecv.at[fk], at, k, lambda s: skip + s * (JL * width) + at.start
+        )
+
+    def taken_at(c, j, r):
+        start, width = ROW_PARTS[c]
+        return NS * start + j * width + r
+
+    loop(2, field_row)
     pl.semaphore_wait(barrier, (NS - 1) + (nd - 1))
-    first_at = [pl.ds(first * PAIR, count * PAIR) for first, count, _ in PARTS]
-    for c, at in enumerate(first_at):
-        exchange(fsend.at[0], frecv.at[0], at, c, lambda e: e * FULL + at.start)
-
+
+    def field_pair(pair):
+        send_rows(0, pair, 0, pair)
+        loop(2, lambda t: field_row(2 * pair + 2 + t))
+
+    loop(HB - 1, field_pair)
+    send_rows(0, HB - 1, 0, HB - 1)
+    send_rows(0, HB, 1)
+
+    ready(6, OPERANDS)
     row16 = lax.broadcasted_iota(jnp.int32, (16, 128), 0)
     order = jnp.where(row16 >= HB, ROWS - 1 - 5 * me - (row16 - HB), 5 * me + row16).astype(F32)
     order2 = order * order
@@ -383,8 +437,9 @@
 
     loop(JL, fire_columns)
 
-    def analyse(c, k, hk, table, rows_of):
+    def analyse(c, k, hk, table):
         first, count, height = PARTS[c]
+        rows_of = rows_of_order(c)
 
         def one(i):
             low = mm_nn(table[i][:, 0:ROWS], rows_of(0, i))
@@ -405,15 +460,18 @@
             hsend[c].at[hk], hrecv[c].at[hk], pl.ds(0, height), k, lambda e: e * height
         )
 
-    def first_rows(h, i):
-        a = taken[pl.ds(i * 640 + h, ROWS, stride=4), :]
-        b = taken[pl.ds(i * 640 + 2 + h, ROWS, stride=4), :]
-        return wide(a, b).astype(BF16)
-
-    def later_rows(h, i):
-        a = taken[pl.ds(h * HB + i, ROWS, stride=2 * MM), :]
-        b = taken[pl.ds(MM + h * HB + i, ROWS, stride=2 * MM), :]
-        return wide(a, b).astype(BF16)
+    def rows_of_order(c):
+        first, count, _ = PARTS[c]
+        _, width = ROW_PARTS[c]
+
+        def rows(h, i):
+            at = taken_at(c, 0, h * count + i - first)
+            return wide(
+                taken[pl.ds(at, ROWS, stride=width), :],
+                taken[pl.ds(at + 2 * count, ROWS, stride=width), :],
+            ).astype(BF16)
+
+        return rows
 
     def mix_degrees(c, hk_in, k_in, hk_out, k_out, backward):
         first, count, height = PARTS[c]
@@ -484,6 +542,7 @@
 
     def synthesise(c, hk, k_in, table):
         first, count, height = PARTS[c]
+        _, width = ROW_PARTS[c]
         arrived(
             hsend[c].at[hk], hrecv[c].at[hk], pl.ds(0, height), k_in, lambda s: s * height
         )
@@ -510,42 +569,48 @@
             high = mm_tn(
                 table[HB + i][:, 0:ROWS], jnp.concatenate(seconds + highs, axis=0).astype(BF16)
             )
-            made[pl.ds(i, ROWS, stride=2 * MM), :] = low[:, 0:128]
-            made[pl.ds(MM + i, ROWS, stride=2 * MM), :] = low[:, 128:256]
-            made[pl.ds(HB + i, ROWS, stride=2 * MM), :] = high[:, 0:128]
-            made[pl.ds(MM + HB + i, ROWS, stride=2 * MM), :] = high[:, 128:256]
+            for p in range(2):
+                lane = slice(p * 128, (p + 1) * 128)
+                at = taken_at(c, 0, p * 2 * count + i - first)
+                made[pl.ds(at, ROWS, stride=width), :] = low[:, lane]
+                made[pl.ds(at + count, ROWS, stride=width), :] = high[:, lane]
 
         loop(first + count, one, first)
 
-    def pair_rows(c):
-        return pl.ds(pl.multiple_of(c * PAIR, 8), PAIR)
-
-    def send_pair(fk, k, c):
-        exchange(fsend.at[fk], frecv.at[fk], pair_rows(c), k + c, lambda e: e * FULL + c * PAIR)
-
-    def take_pair(fk, k, c):
-        arrived(fsend.at[fk], frecv.at[fk], pair_rows(c), k + c, lambda s: s * FULL + c * PAIR)
+    def send_back(fk, k, c, pair=None):
+        at = rows_at(c, pair)
+        start, width = ROW_PARTS[c]
+        skip = NS * start - start
+        exchange(
+            fsend.at[fk], frecv.at[fk], at, k, lambda e: skip + e * (JL * width) + at.start
+        )
 
     def from_orders(j, table):
-        pieces = [taken[pl.ds(j * (2 * MM) + r, NS, stride=FULL), :] for r in range(2 * MM)]
+        pieces = []
+        for p in range(2):
+            for h in range(2):
+                for c, (_, count, _) in enumerate(PARTS):
+                    _, width = ROW_PARTS[c]
+                    for i in range(count):
+                        at = taken_at(c, j, (p * 2 + h) * count + i)
+                        pieces.append(taken[pl.ds(at, NS, stride=JL * width), :])
         return mm_nn(table[...], jnp.concatenate(pieces, axis=0).astype(BF16))
 
-    for c, (first, count, _) in enumerate(PARTS):
-        for i in range(first, first + count):
-            at = pl.ds(i * PAIR, PAIR)
-            if i == first:
-                whole(fsend.at[0], frecv.at[0], first_at[c], c).wait_recv()
-
-            def first_block(s):
-                taken[pl.ds(pl.multiple_of(i * 640 + s * PAIR, 8), PAIR), :] = frecv[0, s, at, :].astype(F32)
-
-            loop(NS, first_block)
-        analyse(c, 2 + c, 0, weighted, first_rows)
+    def orders_arrived(fk, k, c):
+        if c == 0:
+            loop(HB, lambda pair: rows_arrived(fk, k + pair, 0, pair))
+        else:
+            rows_arrived(fk, k + HB, 1)
+
     for c in range(2):
-        mix_degrees(c, 0, 2 + c, 1, 4 + c, False)
+        orders_arrived(0, 0, c)
+        analyse(c, 6 + c, 0, weighted)
     for c in range(2):
-        synthesise(c, 1, 4 + c, plain)
-    loop(HB, lambda c: send_pair(1, 6, c))
+        mix_degrees(c, 0, 6 + c, 1, 8 + c, False)
+    synthesise(0, 1, 8, plain)
+    send_back(1, 10, 0)
+    synthesise(1, 1, 9, plain)
+    loop(HB, lambda pair: send_back(1, 11 + pair, 1, pair))
 
     small[...] = jnp.zeros((640, CHAN), F32)
 
@@ -567,16 +632,17 @@
         grad_inner = (normalize_grad(second, factor, grad_second) * inner_slope).astype(BF16)
         small[0:128, :] += mm_tn(row, grad_inner)
         inner_grad[j] = grad_inner
-        spectrum = mm_nn(syn_ref[...], grad_inner)
-        for r in range(2 * MM):
-            made[pl.ds(j * (2 * MM) + r, NS, stride=FULL), :] = spectrum[r * NS : (r + 1) * NS]
-
-    def middle_pair(c):
-        take_pair(1, 6, c)
-        loop(2, lambda t: middle_row(2 * c + t))
-        send_pair(2, 11, c)
+        to_orders(j, syn_ref, grad_inner)
+
+    rows_arrived(1, 10, 0)
+
+    def middle_pair(pair):
+        rows_arrived(1, 11 + pair, 1, pair)
+        loop(2, lambda t: middle_row(2 * pair + t))
+        send_rows(2, 16 + pair, 0, pair)
 
     loop(HB, middle_pair)
+    send_rows(2, 16 + HB, 1)
 
     def small_source(t):
         return small.at[pl.ds(pl.multiple_of(t * pr, 8), pr), :]
@@ -584,9 +650,9 @@
     spread("dp", nd, dp, 0, small_source, small_in, True)
     small_in[dp] = small[pl.ds(pl.multiple_of(dp * pr, 8), pr), :]
 
-    loop(HB, lambda c: take_pair(2, 11, c))
     for c in range(2):
-        analyse(c, 16 + c, 2, plain, later_rows)
+        orders_arrived(2, 16, c)
+        analyse(c, 22 + c, 2, plain)
 
     spread("dp", nd, dp, 0, small_source, small_in, False)
     piece1[...] = total(small_in, nd)
@@ -609,7 +675,7 @@
     loop(OWNERS, to_owner)
 
     for c in range(2):
-        mix_degrees(c, 2, 16 + c, 3, 18 + c, True)
+        mix_degrees(c, 2, 22 + c, 3, 24 + c, True)
 
     def owner_out(t, slot):
         return pltpu.make_async_remote_copy(
@@ -643,16 +709,99 @@
 
     loop(HB, weight_gradient)
 
-    def narrow_spec(t):
-        spec_send[t] = spec[pl.ds(pl.multiple_of(t * sr, 16), sr), :].astype(BF16)
-
-    loop(nd, narrow_spec)
-    spread("dp", nd, dp, 3, lambda t: spec_send.at[t], spec_in, True)
-    spec_in[dp] = spec_send[dp]
-
-    for c in range(2):
-        synthesise(c, 3, 18 + c, weighted)
-    loop(HB, lambda c: send_pair(3, 20, c))
+    half = 1280
+    nq = nd // 2
+    core = lax.rem(dp, 2)
+    chip = dp // 2
+
+    def to_core(source, target, k):
+        return pltpu.make_async_remote_copy(
+            src_ref=source,
+            dst_ref=target,
+            send_sem=dsend.at[k],
+            recv_sem=drecv.at[k],
+            device_id={"dp": dp + 1 - 2 * core},
+            device_id_type=MESH,
+        )
+
+    def to_chips(source_of, recv, k, start):
+        if nq <= 1:
+            return
+        if not start:
+            done = to_core(recv.at[pl.ds(0, nq - 1)], recv.at[pl.ds(0, nq - 1)], k)
+            done.wait_recv()
+            done.wait_send()
+            return
+
+        def one(o):
+            t = lax.rem(chip + o, nq)
+            pltpu.make_async_remote_copy(
+                src_ref=source_of(t),
+                dst_ref=recv.at[chip],
+                send_sem=dsend.at[k],
+                recv_sem=drecv.at[k],
+                device_id={"dp": 2 * t + core},
+                device_id_type=MESH,
+            ).start()
+
+        loop(nq, one, 1)
+
+    def spec_first():
+        if nd == 1:
+            return
+        other = pl.multiple_of((1 - core) * half, 128)
+        spec_send[...] = spec[pl.ds(other, half), :].astype(BF16)
+        to_core(spec_send, spec_core, 3).start()
+
+    def spec_second():
+        if nd == 1:
+            return
+        to_core(spec_send, spec_core, 3).wait_recv()
+        mine = pl.multiple_of(core * half, 128)
+
+        def add(t):
+            at = pl.ds(pl.multiple_of(t * sr, 16), sr)
+            both = spec[pl.ds(pl.multiple_of(mine + t * sr, 16), sr), :] + spec_core[at, :].astype(F32)
+            spec_mine[t] = both.astype(BF16)
+
+        loop(nq, add)
+        to_chips(lambda t: spec_mine.at[t], spec_in, 5, True)
+        spec_in[chip] = spec_mine[chip]
+
+    def spec_third():
+        if nd == 1:
+            return
+        to_core(spec_send, spec_core, 3).wait_send()
+        to_chips(lambda t: spec_mine.at[t], spec_in, 5, False)
+        spec_piece[...] = total(spec_in, nq).astype(BF16)
+        to_chips(lambda t: spec_piece, spec_all.at[core], 6, True)
+        spec_all[core, chip] = spec_piece[...]
+
+    def spec_fourth():
+        if nd == 1:
+            return
+        to_chips(lambda t: spec_piece, spec_all.at[core], 6, False)
+        to_core(spec_all.at[core], spec_all.at[core], 7).start()
+
+    def spec_fifth():
+        if nd == 1:
+            spectral_out[...] = spec[...]
+            return
+        to_core(spec_all.at[core], spec_all.at[1 - core], 7).wait()
+
+        def widen(t):
+            for c in range(2):
+                at = pl.ds(pl.multiple_of(c * half + t * sr, 16), sr)
+                spectral_out[at, :] = spec_all[c, t].astype(F32)
+
+        loop(nq, widen)
+
+    spec_first()
+    synthesise(0, 3, 24, weighted)
+    send_back(3, 26, 0)
+    spec_second()
+    synthesise(1, 3, 25, weighted)
+    loop(HB, lambda pair: send_back(3, 27 + pair, 1, pair))
 
     def counted(ref, count, k):
         return pltpu.make_async_remote_copy(
@@ -678,18 +827,20 @@
     spread("dp", nd, dp, 4, lambda t: piece2, small_all, True)
     small_all[dp] = piece2[...]
 
-    spread("dp", nd, dp, 3, lambda t: spec_send.at[t], spec_in, False)
-    spec_piece[...] = total(spec_in, nd).astype(BF16)
-    spread("dp", nd, dp, 5, lambda t: spec_piece, spec_all, True)
-    spec_all[dp] = spec_piece[...]
-
-    for c, at in enumerate(first_at):
-        whole(fsend.at[0], frecv.at[0], at, c).wait_send()
-    for k, hk in ((2, 0), (4, 1), (16, 2), (18, 3)):
+    spec_third()
+
+    for k, fk in ((0, 0), (16, 2)):
+        loop(HB, lambda pair: whole(fsend.at[fk], frecv.at[fk], rows_at(0, pair), k + pair).wait_send())
+        whole(fsend.at[fk], frecv.at[fk], rows_at(1), k + HB).wait_send()
+    for k, hk in ((6, 0), (8, 1), (22, 2), (24, 3)):
         for c, (_, _, height) in enumerate(PARTS):
             whole(hsend[c].at[hk], hrecv[c].at[hk], pl.ds(0, height), k + c).wait_send()
-    for k, fk in ((6, 1), (11, 2)):
-        loop(HB, lambda c: whole(fsend.at[fk], frecv.at[fk], pair_rows(c), k + c).wait_send())
+
+    def back_sent(k, fk):
+        whole(fsend.at[fk], frecv.at[fk], rows_at(0), k).wait_send()
+        loop(HB, lambda pair: whole(fsend.at[fk], frecv.at[fk], rows_at(1, pair), k + 1 + pair).wait_send())
+
+    back_sent(10, 1)
 
     tab_mine[...] = jnp.zeros((32, CHAN), F32)
 
@@ -699,16 +850,20 @@
         field_out[j] = grad.astype(BF16)
         tab_mine[...] += mm_exact(fire_t[j], grad)
 
-    def last_pair(c):
-        take_pair(3, 20, c)
-        loop(2, lambda t: last_row(2 * c + t))
-
-    loop(HB, last_pair)
+    rows_arrived(3, 26, 0)
+
+    def last_pair(pair):
+        rows_arrived(3, 27 + pair, 1, pair)
+        loop(2, lambda t: last_row(2 * pair + t))
+
+    loop(3, last_pair)
+    spec_fourth()
+    loop(HB, last_pair, 3)
     tab_mine[0:8, :] = tab_mine[0:8, :] + tab_mine[8:16, :] + tab_mine[16:24, :]
-    spread("space", NS, me, 6, lambda t: tab_mine.at[0:8], tab_space, True)
+    spread("space", NS, me, 8, lambda t: tab_mine.at[0:8], tab_space, True)
     tab_space[me] = tab_mine[0:8, :]
 
-    loop(HB, lambda c: whole(fsend.at[3], frecv.at[3], pair_rows(c), 20 + c).wait_send())
+    back_sent(26, 3)
     spread("dp", nd, dp, 4, lambda t: piece2, small_all, False)
     flat_small = [small_all[t, g] for t in range(nd) for g in range(OWNERS)]
     flat_small = jnp.concatenate(flat_small, axis=0)
@@ -716,19 +871,26 @@
     up_out[:, 0:128] = flat_small[128:256]
     up_out[:, 128:256] = flat_small[256:384]
     down_out[...] = flat_small[384:640]
-    spread("dp", nd, dp, 5, lambda t: spec_piece, spec_all, False)
-
-    def copy_spec(t):
-        spectral_out[pl.ds(pl.multiple_of(t * sr, 16), sr), :] = spec_all[t]
-
-    loop(nd, copy_spec)
-
-    spread("space", NS, me, 6, lambda t: tab_mine.at[0:8], tab_space, False)
+    spec_fifth()
+
+    spread("space", NS, me, 8, lambda t: tab_mine.at[0:8], tab_space, False)
     tab_sum[...] = total(tab_space, NS)
-    spread("dp", nd, dp, 7, lambda t: tab_sum, tab_dp, True)
+    spread("dp", nd, dp, 9, lambda t: tab_sum, tab_dp, True)
     tab_dp[dp] = tab_sum[...]
-    spread("dp", nd, dp, 7, lambda t: tab_sum, tab_dp, False)
+    spread("dp", nd, dp, 9, lambda t: tab_sum, tab_dp, False)
     table_out[...] = total(tab_dp, nd)
+
+
+def hand_over(*refs):
+    sems = refs[-1]
+    count = len(refs) // 2
+    copies = [
+        pltpu.make_async_copy(refs[n], refs[count + n], sems.at[n]) for n in range(count)
+    ]
+    for copy in copies:
+        copy.start()
+    for copy in copies:
+        copy.wait()
 
 
 def shards(
@@ -745,36 +907,40 @@
     down_weight,
 ):
     ana, anat, syn, synt, start, waves = (jnp.asarray(t) for t in constant_tables())
-    pr, sr = 640 // nd, 2560 // nd
+    nq = max(nd // 2, 1)
+    pr, sr = 640 // nd, 1280 // nq
     operands = (
         state_field[0],
-        cotangent[0],
         fire_cells,
         fire_kinds,
         fire_heat,
         forcing_table,
+        ana,
+        start,
+        waves,
         spectral_weight.reshape(4 * HB, CHAN, CHAN),
+        cotangent[0],
+        synt,
         skip_weight,
         up_weight,
         down_weight,
-        ana,
+        syn,
         anat,
-        syn,
-        synt,
-        start,
-        waves,
     )
     vmem = pl.BlockSpec(memory_space=pltpu.VMEM)
     out_shape = (
         jax.ShapeDtypeStruct((JL, NLON, CHAN), BF16),
-        jax.ShapeDtypeStruct((2560, CHAN), BF16),
+        jax.ShapeDtypeStruct((2560, CHAN), F32),
         jax.ShapeDtypeStruct((CHAN, CHAN), F32),
         jax.ShapeDtypeStruct((CHAN, HIDDEN), F32),
         jax.ShapeDtypeStruct((HIDDEN, CHAN), F32),
         jax.ShapeDtypeStruct((FORCE, CHAN), F32),
     )
     (_, ca, ha), (_, cb, hb) = PARTS
-    scratch = [
+    outside = pl.BlockSpec(memory_space=pltpu.HBM)
+    scratch = [pltpu.VMEM(v.shape, v.dtype) for v in operands]
+    scratch += [
+        pltpu.SemaphoreType.DMA((OPERANDS,)),
         pltpu.VMEM((JL, NLON, CHAN), F32),
         pltpu.VMEM((JL, NLON, CHAN), F32),
         pltpu.VMEM((JL, NLON, CHAN), BF16),
@@ -809,23 +975,25 @@
         pltpu.VMEM((OWNERS, pr // OWNERS, CHAN), F32),
         pltpu.VMEM((nd, OWNERS, pr // OWNERS, CHAN), F32),
         pltpu.VMEM((2560, CHAN), F32),
-        pltpu.VMEM((nd, sr, CHAN), BF16),
-        pltpu.VMEM((nd, sr, CHAN), BF16),
+        pltpu.VMEM((1280, CHAN), BF16),
+        pltpu.VMEM((1280, CHAN), BF16),
+        pltpu.VMEM((nq, sr, CHAN), BF16),
+        pltpu.VMEM((nq, sr, CHAN), BF16),
         pltpu.VMEM((sr, CHAN), BF16),
-        pltpu.VMEM((nd, sr, CHAN), BF16),
+        pltpu.VMEM((2, nq, sr, CHAN), BF16),
         pltpu.VMEM((32, CHAN), F32),
         pltpu.VMEM((NS, FORCE, CHAN), F32),
         pltpu.VMEM((FORCE, CHAN), F32),
         pltpu.VMEM((nd, FORCE, CHAN), F32),
-        pltpu.SemaphoreType.DMA((25,)),
-        pltpu.SemaphoreType.DMA((25,)),
-        pltpu.SemaphoreType.DMA((8,)),
-        pltpu.SemaphoreType.DMA((8,)),
+        pltpu.SemaphoreType.DMA((32,)),
+        pltpu.SemaphoreType.DMA((32,)),
+        pltpu.SemaphoreType.DMA((10,)),
+        pltpu.SemaphoreType.DMA((10,)),
     ]
-    field, spectral, skip, up, down, table = pl.pallas_call(
+    results = pl.pallas_call(
         functools.partial(step_kernel, nd),
         out_shape=out_shape,
-        in_specs=[vmem] * len(operands),
+        in_specs=[outside] * len(operands),
         out_specs=(vmem,) * len(out_shape),
         scratch_shapes=scratch,
         compiler_params=pltpu.CompilerParams(
@@ -833,8 +1001,16 @@
         ),
         name="step",
     )(*operands)
-    spectral = spectral.reshape(spectral_weight.shape).astype(F32)
-    return (field[None], spectral, skip, up, down, table)
+    hbm = pl.BlockSpec(memory_space=pl.ANY)
+    field, spectral, skip, up, down, table = pl.pallas_call(
+        hand_over,
+        out_shape=out_shape,
+        in_specs=[vmem] * len(out_shape),
+        out_specs=(hbm,) * len(out_shape),
+        scratch_shapes=[pltpu.SemaphoreType.DMA((len(out_shape),))],
+        name="hand_over",
+    )(*results)
+    return (field[None], spectral.reshape(spectral_weight.shape), skip, up, down, table)
 
 
 def solution(mesh):

time: 161 us -> 153 us (0.950)
  local copies, waits for them, and re-layouts: 3.45 us -> 0 us
  Pallas kernels: 155 us -> 152 us
  other arithmetic: 2.36 us -> 0 us
    pallas_call x1, Pallas kernels: 155 us -> 149 us  [shards(): pl.pallas_call(functools.partial(step_kernel, nd), out_shape=out_shape, i...]
    unnamed x15 -> x0, local copies, waits for them, and re-layouts: 3.45 us -> none
    pallas_call x0 -> x1, Pallas kernels: none -> 3.08 us  [shards(): pl.pallas_call(hand_over, out_shape=out_shape, in_specs=[vmem] * len(out_...]
    convert_element_type x1 -> x0, other arithmetic: 2.36 us -> none  [shards(): spectral = spectral.reshape(spectral_weight.shape).astype(F32)]
where the time goes in v3:
time: 153 us
  Pallas kernels  152 us (99%)
    pallas_call x1, Pallas kernels, shards(): pl.pallas_call(functools.partial(step_kernel, nd), out_shape=out_shape, i...  149 us
    pallas_call x1, Pallas kernels, shards(): pl.pallas_call(hand_over, out_shape=out_shape, in_specs=[vmem] * len(out_...  3.08 us

profile of v3, /device:TPU:1, one launch (start us, length us, event | category | flops | bytes accessed | tf_op | source)
XLA Modules:
  0.0 153.0 jit_solution(17281391689778241048)
XLA Ops:
  0.6 149.3 %step.1 = (bf16[10,320,128]{2,1,0:T(8,128)(2,1)}, f32[2560,128]{1,0:T(8,128)}, f32[128,128]{1,0:T(8,128)}, f32[128,256]{1,0:T(8,128)}, f32[256,128]{1,0:T(8,128)}, /*index=5*/f32[8,128]{1,0:T(8,128)}) custom-call(bf16[10,320,128]{2,1,0:T(8,128)(2,1)} %bitcast.5, s32[1,256]{1,0:T(1,128)} %refs_1_.1, s32[1,256]{1,0:T(1,128)} %refs_2_.1, f32[1,256]{1,0:T(1,128)} %refs_3_.1, ...), custom_call_target="tpu_custom_call" | custom-call | tf_op jit(solution)/shard_map/step/pallas_call | solution.py:993
  149.9 3.1 %hand_over.1 = (bf16[10,320,128]{2,1,0:T(8,128)(2,1)}, f32[2560,128]{1,0:T(8,128)}, f32[128,128]{1,0:T(8,128)}, f32[128,256]{1,0:T(8,128)}, f32[256,128]{1,0:T(8,128)}, /*index=5*/f32[8,128]{1,0:T(8,128)}) custom-call(bf16[10,320,128]{2,1,0:T(8,128)(2,1)} %get-tuple-element.18.refs_0_, f32[2560,128]{1,0:T(8,128)} %get-tuple-element.19.refs_1_, ...), custom_call_target="tpu_custom_call" | custom-call | tf_op jit(solution)/shard_map/hand_over/pallas_call | solution.py:1005

commit v4 on v3

--- a/solution.py
+++ b/solution.py
@@ -24,6 +24,7 @@
 PARTS = ((0, 2, 40), (2, 3, 64))
 ROW_PARTS = ((0, 8), (80, 12))
 OPERANDS = 16
+FAR_FIRST = (4, 12, 5, 11, 3, 13, 6, 10, 2, 14, 7, 9, 1, 15, 8)
 OWNERS = 5
 EPSILON = 1e-06
 MESH = pl.DeviceIdType.MESH
@@ -236,10 +237,10 @@
 
     def exchange(send, recv, at, k, source):
         count = at.size
-
-        def one(o):
+        for e in range(NS):
+            send[e, at, :] = made[pl.ds(pl.multiple_of(source(e), 8), count), :].astype(BF16)
+        for o in FAR_FIRST:
             e = lax.rem(me + o, NS)
-            send[e, at, :] = made[pl.ds(pl.multiple_of(source(e), 8), count), :].astype(BF16)
             pltpu.make_async_remote_copy(
                 src_ref=send.at[e, at],
                 dst_ref=recv.at[me, at],
@@ -248,9 +249,7 @@
                 device_id={"space": e},
                 device_id_type=MESH,
             ).start()
-
-        loop(NS, one, 1)
-        recv[me, at, :] = made[pl.ds(pl.multiple_of(source(me), 8), count), :].astype(BF16)
+        recv[me, at, :] = send[me, at, :]
 
     def whole(send, recv, at, k):
         return pltpu.make_async_remote_copy(
@@ -265,10 +264,8 @@
     def arrived(send, recv, at, k, target):
         whole(send, recv, at, k).wait_recv()
 
-        def one(s):
+        for s in range(NS):
             taken[pl.ds(pl.multiple_of(target(s), 8), at.size), :] = recv[s, at, :].astype(F32)
-
-        loop(NS, one)
 
     def spread(axis, count, mine, k, source_of, recv, start):
         if count == 1:

time: 153 us -> 148 us (0.967)
  Pallas kernels: 152 us -> 147 us
    pallas_call x1, Pallas kernels: 149 us -> 144 us  [shards(): pl.pallas_call(functools.partial(step_kernel, nd), out_shape=out_shape, i...]
where the time goes in v4:
time: 148 us
  Pallas kernels  147 us (99%)
    pallas_call x1, Pallas kernels, shards(): pl.pallas_call(functools.partial(step_kernel, nd), out_shape=out_shape, i...  144 us
    pallas_call x1, Pallas kernels, shards(): pl.pallas_call(hand_over, out_shape=out_shape, in_specs=[vmem] * len(out_...  3.08 us

profile of v4, /device:TPU:1, one launch (start us, length us, event | category | flops | bytes accessed | tf_op | source)
XLA Modules:
  0.0 147.5 jit_solution(4680030926995948209)
XLA Ops:
  0.6 143.8 %step.1 = (bf16[10,320,128]{2,1,0:T(8,128)(2,1)}, f32[2560,128]{1,0:T(8,128)}, f32[128,128]{1,0:T(8,128)}, f32[128,256]{1,0:T(8,128)}, f32[256,128]{1,0:T(8,128)}, /*index=5*/f32[8,128]{1,0:T(8,128)}) custom-call(bf16[10,320,128]{2,1,0:T(8,128)(2,1)} %bitcast.5, s32[1,256]{1,0:T(1,128)} %refs_1_.1, s32[1,256]{1,0:T(1,128)} %refs_2_.1, f32[1,256]{1,0:T(1,128)} %refs_3_.1, ...), custom_call_target="tpu_custom_call" | custom-call | tf_op jit(solution)/shard_map/step/pallas_call | solution.py:990
  144.5 3.1 %hand_over.1 = (bf16[10,320,128]{2,1,0:T(8,128)(2,1)}, f32[2560,128]{1,0:T(8,128)}, f32[128,128]{1,0:T(8,128)}, f32[128,256]{1,0:T(8,128)}, f32[256,128]{1,0:T(8,128)}, /*index=5*/f32[8,128]{1,0:T(8,128)}) custom-call(bf16[10,320,128]{2,1,0:T(8,128)(2,1)} %get-tuple-element.18.refs_0_, f32[2560,128]{1,0:T(8,128)} %get-tuple-element.19.refs_1_, ...), custom_call_target="tpu_custom_call" | custom-call | tf_op jit(solution)/shard_map/hand_over/pallas_call | solution.py:1002

commit v5 on v4

--- a/solution.py
+++ b/solution.py
@@ -119,6 +119,11 @@
         return carry
 
     lax.fori_loop(start, count, step, 0)
+
+
+def unrolled(count, body, start=0):
+    for index in range(start, count):
+        body(index)
 
 
 def rounded(v):
@@ -294,7 +299,7 @@
                 device_id_type=MESH,
             ).start()
 
-        loop(count, one, 1)
+        unrolled(count, one, 1)
 
     def total(recv, count):
         value = recv[0].astype(F32)
@@ -369,7 +374,7 @@
 
     def field_pair(pair):
         send_rows(0, pair, 0, pair)
-        loop(2, lambda t: field_row(2 * pair + 2 + t))
+        unrolled(2, lambda t: field_row(2 * pair + 2 + t))
 
     loop(HB - 1, field_pair)
     send_rows(0, HB - 1, 0, HB - 1)
@@ -452,7 +457,7 @@
                     made[pl.ds(at + 5 * count, NS, stride=height), :] = jnp.where(row16 >= me, ll, hh)
                     extra[pl.ds(p * 32 + i * HB + ii, NS, stride=64), :] = rounded(hh)
 
-        loop(first + count, one, first)
+        unrolled(first + count, one, first)
         exchange(
             hsend[c].at[hk], hrecv[c].at[hk], pl.ds(0, height), k, lambda e: e * height
         )
@@ -572,7 +577,7 @@
                 made[pl.ds(at, ROWS, stride=width), :] = low[:, lane]
                 made[pl.ds(at + count, ROWS, stride=width), :] = high[:, lane]
 
-        loop(first + count, one, first)
+        unrolled(first + count, one, first)
 
     def send_back(fk, k, c, pair=None):
         at = rows_at(c, pair)
@@ -635,7 +640,7 @@
 
     def middle_pair(pair):
         rows_arrived(1, 11 + pair, 1, pair)
-        loop(2, lambda t: middle_row(2 * pair + t))
+        unrolled(2, lambda t: middle_row(2 * pair + t))
         send_rows(2, 16 + pair, 0, pair)
 
     loop(HB, middle_pair)
@@ -851,7 +856,7 @@
 
     def last_pair(pair):
         rows_arrived(3, 27 + pair, 1, pair)
-        loop(2, lambda t: last_row(2 * pair + t))
+        unrolled(2, lambda t: last_row(2 * pair + t))
 
     loop(3, last_pair)
     spec_fourth()

time: 148 us -> 146 us (0.986)
  Pallas kernels: 147 us -> 145 us
    pallas_call x1, Pallas kernels: 144 us -> 142 us  [shards(): pl.pallas_call(functools.partial(step_kernel, nd), out_shape=out_shape, i...]
where the time goes in v5:
time: 146 us
  Pallas kernels  145 us (99%)
    pallas_call x1, Pallas kernels, shards(): pl.pallas_call(functools.partial(step_kernel, nd), out_shape=out_shape, i...  142 us
    pallas_call x1, Pallas kernels, shards(): pl.pallas_call(hand_over, out_shape=out_shape, in_specs=[vmem] * len(out_...  3.08 us

profile of v5, /device:TPU:1, one launch (start us, length us, event | category | flops | bytes accessed | tf_op | source)
XLA Modules:
  0.0 145.7 jit_solution(13644493469780529757)
XLA Ops:
  0.6 141.8 %step.1 = (bf16[10,320,128]{2,1,0:T(8,128)(2,1)}, f32[2560,128]{1,0:T(8,128)}, f32[128,128]{1,0:T(8,128)}, f32[128,256]{1,0:T(8,128)}, f32[256,128]{1,0:T(8,128)}, /*index=5*/f32[8,128]{1,0:T(8,128)}) custom-call(bf16[10,320,128]{2,1,0:T(8,128)(2,1)} %bitcast.5, s32[1,256]{1,0:T(1,128)} %refs_1_.1, s32[1,256]{1,0:T(1,128)} %refs_2_.1, f32[1,256]{1,0:T(1,128)} %refs_3_.1, ...), custom_call_target="tpu_custom_call" | custom-call | tf_op jit(solution)/shard_map/step/pallas_call | solution.py:995
  142.4 3.1 %hand_over.1 = (bf16[10,320,128]{2,1,0:T(8,128)(2,1)}, f32[2560,128]{1,0:T(8,128)}, f32[128,128]{1,0:T(8,128)}, f32[128,256]{1,0:T(8,128)}, f32[256,128]{1,0:T(8,128)}, /*index=5*/f32[8,128]{1,0:T(8,128)}) custom-call(bf16[10,320,128]{2,1,0:T(8,128)(2,1)} %get-tuple-element.18.refs_0_, f32[2560,128]{1,0:T(8,128)} %get-tuple-element.19.refs_1_, ...), custom_call_target="tpu_custom_call" | custom-call | tf_op jit(solution)/shard_map/hand_over/pallas_call | solution.py:1007
